TPU v7x, 32 devices: a whole 2x2x4 slice. The times are simulated.
32 devices in a mesh: ctx: 16 (over z, y, core), heads: 2 (over x).
Axes of the slice: x: 2, y: 2, z: 4, core: 2. Of those that a mesh axis runs over, the one named last changes fastest.
Arguments:
- activations: bfloat16 [5376, 16384], P('heads', 'ctx'), may hold values from -6 to 6
- frozen_query_rows: bfloat16 [16384, 4096], P('ctx', 'heads'), may hold values from -100 to 100
- frozen_key_rows: bfloat16 [16384, 2048], P('ctx', 'heads'), may hold values from -6 to 6
- frozen_value_rows: bfloat16 [16384, 2048], P('ctx', 'heads'), may hold values from -6 to 6
- output_gradient: bfloat16 [16384, 4096], P('ctx', 'heads'), may hold values from -0.5 to 0.5
- query_down_weight: bfloat16 [5376, 16], P('heads'), may hold values from -0.078125 to 0.078125
- query_up_weight: bfloat16 [16, 4096], P(None, 'heads'), may hold values from -0.0390625 to 0.0390625
- key_down_weight: bfloat16 [5376, 16], P('heads'), may hold values from -0.078125 to 0.078125
- key_up_weight: bfloat16 [16, 2048], P(None, 'heads'), may hold values from -0.0390625 to 0.0390625
- value_down_weight: bfloat16 [5376, 16], P('heads'), may hold values from -0.078125 to 0.078125
- value_up_weight: bfloat16 [16, 2048], P(None, 'heads'), may hold values from -0.0390625 to 0.0390625
Outputs:
- query_down_gradient: float32 [5376, 16], P('heads')
- query_up_gradient: float32 [16, 4096], P(None, 'heads')
- key_down_gradient: float32 [5376, 16], P('heads')
- key_up_gradient: float32 [16, 2048], P(None, 'heads')
- value_down_gradient: float32 [5376, 16], P('heads')
- value_up_gradient: float32 [16, 2048], P(None, 'heads')
All inputs are finite; a program needn't handle non-finite values.
Results may differ from a plain program's by a relative error of at most 0.0098.
Values may be sent and summed in bfloat16 or wider, within the bound.
No kernel may reach another device: no remote copies, remote signals or barrier semaphores. Data moves between devices by JAX's collectives and lax.ppermute only.
A program may use at most 256 MiB of HBM per device.

v0:
```python
import functools

import jax
import jax.numpy as jnp
from jax import lax
from jax.experimental import pallas as pl
from jax.experimental.pallas import tpu as pltpu
from jax.sharding import PartitionSpec as P


HEAD_WIDTH = 128
ADAPTER_SCALE = 2.0
NEGATIVE = -1e30
LOG2E = 1.4426950408889634
F32 = jnp.float32
BF16 = jnp.bfloat16


def split2(x):
    high = x.astype(BF16)
    return high, (x - high.astype(F32)).astype(BF16)


def split3(x):
    high = x.astype(BF16)
    rest = x - high.astype(F32)
    middle = rest.astype(BF16)
    return high, middle, (rest - middle.astype(F32)).astype(BF16)


def dot_nn(a, b):
    return lax.dot_general(a, b, (((1,), (0,)), ((), ())), preferred_element_type=F32)


def dot_nt(a, b):
    return lax.dot_general(a, b, (((1,), (1,)), ((), ())), preferred_element_type=F32)


def fold8(x, reduce):
    return reduce(x.reshape(x.shape[0] // 8, 8, x.shape[1]), axis=0)


def alternate(*streams):
    waiting = list(streams)
    while waiting:
        for stream in list(waiting):
            if next(stream, None) is None:
                waiting.remove(stream)


def attention_body(
    group,
    rank,
    rows,
    bias_ref,
    rank_ref,
    prior_rank_ref,
    fq_ref,
    do_ref,
    fk_ref,
    pk_ref,
    fv_ref,
    pv_ref,
    uq_ref,
    uk_ref,
    uv_ref,
    inner_ref,
    inner_prior_ref,
    upq_ref,
    upk_ref,
    upv_ref,
    ranks_t,
    ranks,
    k_all,
    v_all,
    k_t,
    dk_acc,
    dv_acc,
    s_scr,
    dp_scr,
    ds_scr,
):
    head = pl.program_id(0)
    own = fk_ref.shape[0]
    width = HEAD_WIDTH
    tiles = own // rows
    half = rows // 2
    lanes = group * rows
    scale = width**-0.5
    factor = scale * LOG2E

    @pl.when(head == 0)
    def _():
        mine = split3(rank_ref[...])
        prior = split3(prior_rank_ref[...])
        blank = jnp.zeros((rank, own), BF16)
        for part in range(3):
            at = part * 3 * rank
            ranks_t[at : at + 3 * rank, own:] = mine[part]
            ranks_t[at : at + rank, :own] = blank
            ranks_t[at + rank : at + 3 * rank, :own] = prior[part]
        ranks[...] = ranks_t[...].astype(F32).T.astype(BF16)
        inner_ref[...] = jnp.zeros_like(inner_ref)
        inner_prior_ref[...] = jnp.zeros_like(inner_prior_ref)

    def stacked(up, kind):
        pieces = []
        for _ in range(3):
            for other in range(3):
                pieces.append(up if other == kind else jnp.zeros_like(up))
        return jnp.concatenate(pieces, axis=0)

    def rank_rows(kind, start, size):
        pieces = [
            ranks_t[(3 * part + kind) * rank : (3 * part + kind + 1) * rank, start : start + size]
            for part in range(3)
        ]
        return jnp.concatenate(pieces, axis=0)

    def merged(x):
        return x[:rank] + x[rank : 2 * rank] + x[2 * rank :]

    def lifted(base, lift):
        return (base.astype(F32) + ADAPTER_SCALE * lift).astype(BF16)

    up_kv = jnp.concatenate([stacked(uk_ref[...], 1), stacked(uv_ref[...], 2)], axis=1)
    up_q = stacked(uq_ref[...], 0)
    for start in range(0, 2 * own, rows):
        lift = dot_nn(ranks[start : start + rows], up_kv)
        source_k, source_v, at = (pk_ref, pv_ref, start) if start < own else (fk_ref, fv_ref, start - own)
        keys = lifted(source_k[at : at + rows], lift[:, :width])
        k_all[start : start + rows] = keys
        k_t[:, start : start + rows] = keys.T
        v_all[start : start + rows] = lifted(source_v[at : at + rows], lift[:, width:])

    key_at = lax.broadcasted_iota(jnp.int32, (rows, lanes), 0)
    lane = lax.broadcasted_iota(jnp.int32, (rows, lanes), 1)
    earlier = key_at > lax.div(lane, group * half) * half + lax.rem(lane, half)
    bias = bias_ref[0]
    state = [{} for _ in range(tiles)]

    def across(x):
        return jnp.concatenate(
            [
                x[part * half : (part + 1) * half, g * width : (g + 1) * width].T
                for part in range(rows // half)
                for g in range(group)
            ],
            axis=1,
        )

    def tile_rows(block, tile):
        start = (block + tile) * rows
        return slice(start, start + rows)

    def tile_bias(block, tile):
        return bias if 0 < tile and block + tile < tiles else None

    def products(block):
        slot = block % 2
        here = slice(block * rows, (block + 1) * rows)
        lift = dot_nn(ranks[own + block * rows : own + (block + 1) * rows], up_q)
        q_t = across(lifted(fq_ref[here], lift))
        do_t = across(do_ref[here])
        highest = None
        for tile in range(tiles):
            scores = dot_nn(k_all[tile_rows(block, tile)], q_t)
            grads = dot_nn(v_all[tile_rows(block, tile)], do_t)
            if tile == 0:
                last = dot_nn(k_all[tile_rows(block, tiles)], q_t)
                scores = jnp.where(earlier, scores + bias, last)
                grads = jnp.where(earlier, grads, dot_nn(v_all[tile_rows(block, tiles)], do_t))
            s_scr[slot, tile] = scores
            dp_scr[slot, tile] = grads
            high = fold8(scores, jnp.max)
            if tile_bias(block, tile) is not None:
                high = high + bias
            highest = high if highest is None else jnp.maximum(highest, high)
            yield True
        state[block].update(q_t=q_t, do_t=do_t, highest=highest)

    def exponents(block):
        slot = block % 2
        top = jnp.max(state[block]["highest"], axis=0, keepdims=True) * factor
        shifted_top = top - bias
        total = dots = None
        for tile in range(tiles):
            minus = top if tile_bias(block, tile) is None else shifted_top
            exponent = jnp.exp2(s_scr[slot, tile] * factor - minus)
            s_scr[slot, tile] = exponent
            one = fold8(exponent, jnp.sum)
            two = fold8(exponent * dp_scr[slot, tile], jnp.sum)
            total = one if total is None else total + one
            dots = two if dots is None else dots + two
            yield True
        inverse = 1.0 / jnp.sum(total, axis=0, keepdims=True)
        state[block].update(
            inverse=inverse,
            row_dots=jnp.sum(dots, axis=0, keepdims=True) * inverse,
            do_scaled=(state[block]["do_t"].astype(F32) * inverse).astype(BF16),
            q_scaled=(state[block]["q_t"].astype(F32) * inverse).astype(BF16),
        )

    def accumulate(acc, block, tile, value):
        fresh = block == 0 or tile == tiles
        if fresh:
            acc[:, tile_rows(block, tile)] = value
        else:
            acc[:, tile_rows(block, tile)] += value

    def gradients(block):
        slot = block % 2
        now = state[block]
        for tile in range(tiles):
            exponent = s_scr[slot, tile]
            grad = exponent * (dp_scr[slot, tile] - now["row_dots"])
            if tile == 0:
                zero = jnp.zeros_like(grad)
                parts = [
                    (0, jnp.where(earlier, grad, zero), jnp.where(earlier, exponent, zero)),
                    (tiles, jnp.where(earlier, zero, grad), jnp.where(earlier, zero, exponent)),
                ]
            else:
                parts = [(tile, grad, exponent)]
            for to, grad, exponent in parts:
                grad_low = grad.astype(BF16)
                ds_scr[slot, to * rows : (to + 1) * rows] = grad_low
                accumulate(dk_acc, block, to, dot_nt(now["q_scaled"], grad_low))
                accumulate(dv_acc, block, to, dot_nt(now["do_scaled"], exponent.astype(BF16)))
            yield True
        window = slice(block * rows, (block + tiles + 1) * rows)
        dq = dot_nn(k_t[:, window], ds_scr[slot]) * (now["inverse"] * scale)
        dq = dq.astype(BF16)
        up = uq_ref[...]
        rank_q = rank_rows(0, own + block * rows, rows)
        for part in range(rows // half):
            at = part * group * half
            tall = jnp.concatenate(
                [dq[:, at + g * half : at + (g + 1) * half] for g in range(group)], axis=0
            )
            start = block * rows + part * half
            inner_ref[:rank, start : start + half] += dot_nn(up, tall)
        for g in range(group):
            head_dq = jnp.concatenate(
                [
                    dq[:, (part * group + g) * half : (part * group + g + 1) * half]
                    for part in range(rows // half)
                ],
                axis=1,
            )
            value = merged(dot_nt(rank_q, head_dq))
            columns = slice(g * width, (g + 1) * width)
            if block == 0:
                upq_ref[:, columns] = value
            else:
                upq_ref[:, columns] += value

    alternate(products(0))
    alternate(products(1), exponents(0))
    for block in range(tiles):
        streams = [gradients(block)]
        if block + 2 < tiles:
            streams.append(products(block + 2))
        if block + 1 < tiles:
            streams.append(exponents(block + 1))
        alternate(*streams)

    for kind, acc, up_ref, out_ref, mult in (
        (1, dk_acc, uk_ref, upk_ref, scale),
        (2, dv_acc, uv_ref, upv_ref, 1.0),
    ):
        low = (acc[...] * mult).astype(BF16)
        out_ref[...] = merged(dot_nt(rank_rows(kind, 0, 2 * own), low))
        inner = dot_nn(up_ref[...], low)
        inner_prior_ref[(kind - 1) * rank : kind * rank, :] += inner[:, :own]
        inner_ref[kind * rank : (kind + 1) * rank, :] += inner[:, own:]


def attention(first, heads, bias, rank_t, prior_rank_t, fq, do, fk, fv, packed, uq, uk, uv, rows=256):
    rank = uq.shape[0]
    own = fk.shape[0]
    width = HEAD_WIDTH
    group = fq.shape[1] // fk.shape[1]
    wide = group * width
    tiles = own // rows
    lanes = group * rows
    whole = lambda h: (0, 0)
    key = lambda h: (0, first + h)
    chunk = lambda h: (0, h)
    in_specs = [
        pl.BlockSpec(memory_space=pltpu.SMEM),
        pl.BlockSpec(rank_t.shape, whole),
        pl.BlockSpec(prior_rank_t.shape, whole),
        pl.BlockSpec((own, wide), key),
        pl.BlockSpec((own, wide), key),
        pl.BlockSpec((own, width), key),
        pl.BlockSpec((own, width), chunk),
        pl.BlockSpec((own, width), key),
        pl.BlockSpec((own, width), lambda h: (0, heads + h)),
        pl.BlockSpec((rank, wide), key),
        pl.BlockSpec((rank, width), key),
        pl.BlockSpec((rank, width), key),
    ]
    out_specs = [
        pl.BlockSpec((3 * rank, own), whole),
        pl.BlockSpec((2 * rank, own), whole),
        pl.BlockSpec((rank, wide), chunk),
        pl.BlockSpec((rank, width), chunk),
        pl.BlockSpec((rank, width), chunk),
    ]
    out_shape = [
        jax.ShapeDtypeStruct((3 * rank, own), F32),
        jax.ShapeDtypeStruct((2 * rank, own), F32),
        jax.ShapeDtypeStruct((rank, heads * wide), F32),
        jax.ShapeDtypeStruct((rank, heads * width), F32),
        jax.ShapeDtypeStruct((rank, heads * width), F32),
    ]
    scratch = [
        pltpu.VMEM((9 * rank, 2 * own), BF16),
        pltpu.VMEM((2 * own, 9 * rank), BF16),
        pltpu.VMEM((2 * own, width), BF16),
        pltpu.VMEM((2 * own, width), BF16),
        pltpu.VMEM((width, 2 * own), BF16),
        pltpu.VMEM((width, 2 * own), F32),
        pltpu.VMEM((width, 2 * own), F32),
        pltpu.VMEM((2, tiles, rows, lanes), F32),
        pltpu.VMEM((2, tiles, rows, lanes), F32),
        pltpu.VMEM((2, (tiles + 1) * rows, lanes), BF16),
    ]
    pairs = heads * group * own * own
    return pl.pallas_call(
        functools.partial(attention_body, group, rank, rows),
        grid=(heads,),
        in_specs=in_specs,
        out_specs=out_specs,
        out_shape=out_shape,
        scratch_shapes=scratch,
        compiler_params=pltpu.CompilerParams(
            dimension_semantics=("arbitrary",), vmem_limit_bytes=67_000_000
        ),
        cost_estimate=pl.CostEstimate(
            flops=10 * pairs * width,
            transcendentals=pairs,
            bytes_accessed=heads * own * width * (4 * group + 8),
        ),
        name="banded_attention",
    )(bias, rank_t, prior_rank_t, fq, do, fk, packed, fv, packed, uq, uk, uv)


def shifted(shard, axis, by):
    length = lax.axis_size(axis)
    pairs = [(i, i + by) for i in range(length) if 0 <= i + by < length]
    return lax.ppermute(shard, axis, pairs)


def exchanged(shard, axis, step):
    length = lax.axis_size(axis)
    return lax.ppermute(shard, axis, [(i, i ^ step) for i in range(length)])


def summed(shard, axis, kind):
    length = lax.axis_size(axis)
    if length & (length - 1):
        return lax.psum(shard, axis)
    step = 1
    while step < length:
        shard = shard + exchanged(shard.astype(kind), axis, step).astype(F32)
        step *= 2
    return shard


def reduced(shard, axis, halvings=2):
    length = lax.axis_size(axis)
    if length & (length - 1):
        return lax.psum(shard, axis)
    index = lax.axis_index(axis)
    steps = [1 << bit for bit in range(length.bit_length() - 1)]
    for step in steps[:halvings]:
        half = shard.shape[1] // 2
        first, second = shard[:, :half], shard[:, half:]
        low = (index // step) % 2 == 0
        kept = jnp.where(low, first, second)
        sent = jnp.where(low, second, first).astype(BF16)
        shard = kept + exchanged(sent, axis, step).astype(F32)
    for step in steps[halvings:]:
        sent = shard.astype(BF16)
        shard = sent.astype(F32) + exchanged(sent, axis, step).astype(F32)
    shard = shard.astype(BF16)
    for step in reversed(steps[:halvings]):
        low = (index // step) % 2 == 0
        other = exchanged(shard, axis, step)
        first, second = jnp.where(low, shard, other), jnp.where(low, other, shard)
        shard = jnp.concatenate([first, second], axis=1)
    return shard.astype(F32)


def portions(heads):
    if heads < 8:
        return [heads]
    return [heads // 4, heads // 4, heads // 2]


def layer(
    activations,
    frozen_query_rows,
    frozen_key_rows,
    frozen_value_rows,
    output_gradient,
    query_down_weight,
    query_up_weight,
    key_down_weight,
    key_up_weight,
    value_down_weight,
    value_up_weight,
):
    rank = query_down_weight.shape[1]
    heads = frozen_key_rows.shape[1] // HEAD_WIDTH
    down = jnp.concatenate([query_down_weight, key_down_weight, value_down_weight], axis=1)
    partial_rank = lax.dot_general(
        down, activations, (((0,), (0,)), ((), ())), preferred_element_type=F32
    )
    rank_t = summed(partial_rank, "heads", F32)
    prior_rank_t = shifted(rank_t[rank:], "ctx", 1)
    prior = []
    first = 0
    for count in portions(heads):
        columns = slice(first * HEAD_WIDTH, (first + count) * HEAD_WIDTH)
        packed = jnp.concatenate(
            [frozen_key_rows[:, columns], frozen_value_rows[:, columns]], axis=1
        )
        prior.append((first, count, shifted(packed, "ctx", 1)))
        first += count
    bias = jnp.where(lax.axis_index("ctx") == 0, NEGATIVE, 0.0).astype(F32).reshape(1)
    inner = inner_prior = None
    ups = []
    for first, count, packed in prior:
        one, one_prior, upq, upk, upv = attention(
            first,
            count,
            bias,
            rank_t,
            prior_rank_t,
            frozen_query_rows,
            output_gradient,
            frozen_key_rows,
            frozen_value_rows,
            packed,
            query_up_weight,
            key_up_weight,
            value_up_weight,
        )
        inner = one if inner is None else inner + one
        inner_prior = one_prior if inner_prior is None else inner_prior + one_prior
        ups.append((upq, upk, upv))
    back = shifted(inner_prior.astype(BF16), "ctx", -1).astype(F32)
    inner = jnp.concatenate([inner[:rank], inner[rank:] + back], axis=0)
    inner = summed(inner, "heads", BF16)
    parts = jnp.concatenate(split2(inner), axis=0)
    down_parts = lax.dot_general(
        parts, activations, (((1,), (1,)), ((), ())), preferred_element_type=F32
    )
    down_t = down_parts[: 3 * rank] + down_parts[3 * rank :]
    pieces = [down_t[kind * rank : (kind + 1) * rank] for kind in range(3)]
    pieces += [jnp.concatenate([up[kind] for up in ups], axis=1) for kind in range(3)]
    packed = ADAPTER_SCALE * jnp.concatenate(pieces, axis=1)
    packed = jnp.pad(packed, ((0, 0), (0, -packed.shape[1] % 512)))
    packed = reduced(packed, "ctx")
    results = []
    start = 0
    for piece in pieces:
        results.append(packed[:, start : start + piece.shape[1]])
        start += piece.shape[1]
    dq, dk, dv, upq, upk, upv = results
    return dq.T, upq, dk.T, upk, dv.T, upv


def solution(mesh):
    in_specs = (
        P("heads", "ctx"),
        P("ctx", "heads"),
        P("ctx", "heads"),
        P("ctx", "heads"),
        P("ctx", "heads"),
        P("heads", None),
        P(None, "heads"),
        P("heads", None),
        P(None, "heads"),
        P("heads", None),
        P(None, "heads"),
    )
    out_specs = (
        P("heads", None),
        P(None, "heads"),
        P("heads", None),
        P(None, "heads"),
        P("heads", None),
        P(None, "heads"),
    )
    return jax.shard_map(layer, mesh=mesh, in_specs=in_specs, out_specs=out_specs, check_vma=False)
```

profile of v0, /device:TPU:0, one launch (start us, length us, event | category | flops | bytes accessed | tf_op | source)
XLA Modules:
  0.0 198.3 jit_solution(17955138085142209006)
XLA Ops:
  0.7 1.2 slice-done.2
  2.2 1.6 pad_maximum_fusion
  3.8 4.0 %collective-permute-start.4 = (bf16[1024,1024]{1,0:T(8,128)(2,1)}, bf16[1024,1024]{1,0:T(8,128)(2,1)}, u32[]{:S(2)}, u32[]{:S(2)}) collective-permute-start(bf16[1024,1024]{1,0:T(8,128)(2,1)} %pad_maximum_fusion), channel_id=1, source_target_pairs={{0,2},{2,4},{4,6},{6,8},{8,10},{10,12},{12,14},{14,16},{16,18},{18... | collective-permute-start | bytes 6291464 | tf_op jit(solution)/shard_map/ppermute | solution.py:353
  8.0 3.3 %collective-permute-start.2 = (bf16[1024,512]{1,0:T(8,128)(2,1)S(1)}, bf16[1024,512]{1,0:T(8,128)(2,1)S(1)}, u32[]{:S(2)}, u32[]{:S(2)}) collective-permute-start(bf16[1024,512]{1,0:T(8,128)(2,1)S(1)} %pad_maximum_fusion.1), channel_id=1, source_target_pairs={{0,2},{2,4},{4,6},{6,8},{8,10},{10,12},{12,14},{14,16},{16,18},{18... | collective-permute-start | bytes 3145736 | tf_op jit(solution)/shard_map/ppermute | solution.py:353
  11.3 1.1 pad_maximum_fusion.2
  12.4 2.9 %collective-permute-start.3 = (bf16[1024,512]{1,0:T(8,128)(2,1)}, bf16[1024,512]{1,0:T(8,128)(2,1)}, u32[]{:S(2)}, u32[]{:S(2)}) collective-permute-start(bf16[1024,512]{1,0:T(8,128)(2,1)} %pad_maximum_fusion.2), channel_id=1, source_target_pairs={{0,2},{2,4},{4,6},{6,8},{8,10},{10,12},{12,14},{14,16},{16,18},{18... | collective-permute-start | bytes 3145736 | tf_op jit(solution)/shard_map/ppermute | solution.py:353
  15.3 1.1 fusion
  16.4 1.6 collective-permute-start
  17.9 6.0 %collective-permute-done = f32[48,1024]{1,0:T(8,128)S(1)} collective-permute-done((f32[48,1024]{1,0:T(8,128)S(1)}, f32[48,1024]{1,0:T(8,128)S(1)}, u32[]{:S(2)}, u32[]{:S(2)}) %collective-permute-start) | collective-permute-done | bytes 196640 | tf_op jit(solution)/shard_map/ppermute | solution.py:358
  24.6 1.7 collective-permute-start.1
  27.9 1.0 copy-done.15
  28.9 25.2 %banded_attention.3 = (f32[48,1024]{1,0:T(8,128)}, f32[32,1024]{1,0:T(8,128)}, f32[16,512]{1,0:T(8,128)}, f32[16,256]{1,0:T(8,128)}, f32[16,256]{1,0:T(8,128)}) custom-call(f32[1]{0:T(128)} %bitcast.bias_ref, f32[48,1024]{1,0:T(8,128)} %copy-done.2, f32[32,1024]{1,0:T(8,128)} %copy-done.16, bf16[1024,2048]{1,0:T(8,128)(2,1)} %fq_ref.5, ...), custom_call_target="tpu_custom_call" | custom-call | flops 5368709120 | bytes 4194304 | tf_op jit(solution)/shard_map/banded_attention/pallas_call | solution.py:331
  54.1 25.4 %banded_attention.4 = (f32[48,1024]{1,0:T(8,128)}, f32[32,1024]{1,0:T(8,128)}, f32[16,512]{1,0:T(8,128)}, f32[16,256]{1,0:T(8,128)}, f32[16,256]{1,0:T(8,128)}) custom-call(f32[1]{0:T(128)} %bitcast.bias_ref, f32[48,1024]{1,0:T(8,128)} %copy-done.2, f32[32,1024]{1,0:T(8,128)} %copy-done.16, bf16[1024,2048]{1,0:T(8,128)(2,1)} %fq_ref.5, ...), custom_call_target="tpu_custom_call" | custom-call | flops 5368709120 | bytes 4194304 | tf_op jit(solution)/shard_map/banded_attention/pallas_call | solution.py:331
  79.4 47.3 %banded_attention.5 = (f32[48,1024]{1,0:T(8,128)}, f32[32,1024]{1,0:T(8,128)}, f32[16,1024]{1,0:T(8,128)}, f32[16,512]{1,0:T(8,128)}, f32[16,512]{1,0:T(8,128)}) custom-call(f32[1]{0:T(128)} %bitcast.bias_ref, f32[48,1024]{1,0:T(8,128)} %copy-done.2, f32[32,1024]{1,0:T(8,128)} %copy-done.16, bf16[1024,2048]{1,0:T(8,128)(2,1)} %fq_ref.5, ...), custom_call_target="tpu_custom_call" | custom-call | flops 10737418240 | bytes 8388608 | tf_op jit(solution)/shard_map/banded_attention/pallas_call | solution.py:331
  126.7 1.1 add_convert_fusion.3
  127.8 1.6 collective-permute-start.5
  129.3 1.1 add_add_fusion
  130.5 28.7 %collective-permute-done.5 = bf16[32,1024]{1,0:T(8,128)(2,1)S(1)} collective-permute-done((bf16[32,1024]{1,0:T(8,128)(2,1)S(1)}, bf16[32,1024]{1,0:T(8,128)(2,1)S(1)}, u32[]{:S(2)}, u32[]{:S(2)}) %collective-permute-start.5) | collective-permute-done | bytes 65568 | tf_op jit(solution)/shard_map/ppermute | solution.py:353
  159.3 1.6 collective-permute-start.6
  160.8 3.1 %collective-permute-done.6 = bf16[48,1024]{1,0:T(8,128)(2,1)S(1)} collective-permute-done((bf16[48,1024]{1,0:T(8,128)(2,1)S(1)}, bf16[48,1024]{1,0:T(8,128)(2,1)S(1)}, u32[]{:S(2)}, u32[]{:S(2)}) %collective-permute-start.6) | collective-permute-done | bytes 98336 | tf_op jit(solution)/shard_map/ppermute | solution.py:358
  164.0 4.3 %fusion.6 = f32[96,2688]{1,0:T(8,128)S(1)} fusion(bf16[2688,1024]{1,0:T(8,128)(2,1)} %param.11, bf16[48,1024]{1,0:T(8,128)(2,1)S(1)} %get-tuple-element.48, bf16[48,1024]{1,0:T(8,128)(2,1)S(1)} %get-tuple-element.47), kind=kOutput, calls=%fused_computation.16 | convolution fusion | flops 528875520 | bytes 6733824 | tf_op jit(solution)/shard_map/dot_general | solution.py:459
  169.5 2.9 %collective-permute-start.7 = (bf16[16,6144]{1,0:T(8,128)(2,1)S(1)}, bf16[16,6144]{1,0:T(8,128)(2,1)S(1)}, u32[]{:S(2)}, u32[]{:S(2)}) collective-permute-start(bf16[16,6144]{1,0:T(8,128)(2,1)S(1)} %select_convert_fusion), channel_id=1, source_target_pairs={{0,2},{2,0},{4,6},{6,4},{8,10},{10,8},{12,14},{14,12},{16,18},{18,... | collective-permute-start | bytes 589832 | tf_op jit(solution)/shard_map/ppermute | solution.py:358
  172.4 1.1 collective-permute-done.7
  173.5 2.2 %collective-permute-start.8 = (bf16[16,3072]{1,0:T(8,128)(2,1)S(1)}, bf16[16,3072]{1,0:T(8,128)(2,1)S(1)}, u32[]{:S(2)}, u32[]{:S(2)}) collective-permute-start(bf16[16,3072]{1,0:T(8,128)(2,1)S(1)} %select_convert_fusion.1), channel_id=1, source_target_pairs={{0,4},{2,6},{4,0},{6,2},{8,12},{10,14},{12,8},{14,10},{16,20},{18,... | collective-permute-start | bytes 294920 | tf_op jit(solution)/shard_map/ppermute | solution.py:358
  175.7 3.3 %collective-permute-done.8 = bf16[16,3072]{1,0:T(8,128)(2,1)S(1)} collective-permute-done((bf16[16,3072]{1,0:T(8,128)(2,1)S(1)}, bf16[16,3072]{1,0:T(8,128)(2,1)S(1)}, u32[]{:S(2)}, u32[]{:S(2)}) %collective-permute-start.8) | collective-permute-done | bytes 98336 | tf_op jit(solution)/shard_map/ppermute | solution.py:358
  179.1 2.3 %collective-permute-start.9 = (bf16[16,3072]{1,0:T(8,128)(2,1)S(1)}, bf16[16,3072]{1,0:T(8,128)(2,1)S(1)}, u32[]{:S(2)}, u32[]{:S(2)}) collective-permute-start(bf16[16,3072]{1,0:T(8,128)(2,1)S(1)} %add_convert_fusion.2), channel_id=1, source_target_pairs={{0,8},{2,10},{4,12},{6,14},{8,0},{10,2},{12,4},{14,6},{16,24},{18,... | collective-permute-start | bytes 294920 | tf_op jit(solution)/shard_map/ppermute | solution.py:358
  181.4 2.6 %collective-permute-done.9 = bf16[16,3072]{1,0:T(8,128)(2,1)S(1)} collective-permute-done((bf16[16,3072]{1,0:T(8,128)(2,1)S(1)}, bf16[16,3072]{1,0:T(8,128)(2,1)S(1)}, u32[]{:S(2)}, u32[]{:S(2)}) %collective-permute-start.9) | collective-permute-done | bytes 98336 | tf_op jit(solution)/shard_map/ppermute | solution.py:358
  184.0 3.1 %collective-permute-start.10 = (bf16[16,3072]{1,0:T(8,128)(2,1)S(1)}, bf16[16,3072]{1,0:T(8,128)(2,1)S(1)}, u32[]{:S(2)}, u32[]{:S(2)}) collective-permute-start(bf16[16,3072]{1,0:T(8,128)(2,1)S(1)} %add_convert_fusion.1), channel_id=1, source_target_pairs={{0,16},{2,18},{4,20},{6,22},{8,24},{10,26},{12,28},{14,30},{16,0},... | collective-permute-start | bytes 294920 | tf_op jit(solution)/shard_map/ppermute | solution.py:358
  187.1 2.6 %collective-permute-done.10 = bf16[16,3072]{1,0:T(8,128)(2,1)S(1)} collective-permute-done((bf16[16,3072]{1,0:T(8,128)(2,1)S(1)}, bf16[16,3072]{1,0:T(8,128)(2,1)S(1)}, u32[]{:S(2)}, u32[]{:S(2)}) %collective-permute-start.10) | collective-permute-done | bytes 98336 | tf_op jit(solution)/shard_map/ppermute | solution.py:358
  189.8 1.5 collective-permute-start.11
  191.2 3.2 %collective-permute-done.11 = bf16[16,3072]{1,0:T(8,128)(2,1)S(1)} collective-permute-done((bf16[16,3072]{1,0:T(8,128)(2,1)S(1)}, bf16[16,3072]{1,0:T(8,128)(2,1)S(1)}, u32[]{:S(2)}, u32[]{:S(2)}) %collective-permute-start.11) | collective-permute-done | bytes 98336 | tf_op jit(solution)/shard_map/ppermute | solution.py:358
  194.6 1.4 collective-permute-done.12
  (81 shorter events, 6.4 us)
Async XLA Ops:
  0.6 1.2 slice-start.2
  0.6 1.5 slice-start.3
  0.7 7.1 %copy-start.1 = (bf16[1024,1024]{1,0:T(8,128)(2,1)S(1)}, bf16[1024,1024]{1,0:T(8,128)(2,1)}, u32[]{:S(2)}) copy-start(bf16[1024,1024]{1,0:T(8,128)(2,1)} %fk_ref.5) | copy-start | bytes 6291460
  2.2 5.6 %copy-start = (bf16[1024,1024]{1,0:T(8,128)(2,1)S(1)}, bf16[1024,1024]{1,0:T(8,128)(2,1)}, u32[]{:S(2)}) copy-start(bf16[1024,1024]{1,0:T(8,128)(2,1)} %fv_ref.5) | copy-start | bytes 6291460
  2.2 13.1 %slice-start = ((s8[5505024]{0:T(1024)(128)(4,1)}), s8[1310720]{0:T(1024)(128)(4,1)S(1)}, s32[]{:S(2)}) async-start(s8[5505024]{0:T(1024)(128)(4,1)} %bitcast.9), calls=%async_computation | async-start | bytes 2621440
  3.8 11.5 %slice-start.1 = ((s8[5505024]{0:T(1024)(128)(4,1)}), s8[4194304]{0:T(1024)(128)(4,1)S(1)}, s32[]{:S(2)}) async-start(s8[5505024]{0:T(1024)(128)(4,1)} %bitcast.9), calls=%async_computation.1 | async-start | bytes 8388608
  3.8 75.7 %collective-permute-start.4 = (bf16[1024,1024]{1,0:T(8,128)(2,1)}, bf16[1024,1024]{1,0:T(8,128)(2,1)}, u32[]{:S(2)}, u32[]{:S(2)}) collective-permute-start(bf16[1024,1024]{1,0:T(8,128)(2,1)} %pad_maximum_fusion), channel_id=1, source_target_pairs={{0,2},{2,4},{4,6},{6,8},{8,10},{10,12},{12,14},{14,16},{16,18},{18... | collective-permute-start | bytes 6291464 | tf_op jit(solution)/shard_map/ppermute | solution.py:353
  7.9 7.3 %copy-start.3 = (bf16[2688,16]{0,1:T(8,128)(2,1)S(1)}, bf16[2688,16]{0,1:T(8,128)(2,1)}, u32[]{:S(2)}) copy-start(bf16[2688,16]{0,1:T(8,128)(2,1)} %param.20) | copy-start | bytes 258052
  7.9 7.3 %copy-start.4 = (bf16[2688,16]{0,1:T(8,128)(2,1)S(1)}, bf16[2688,16]{0,1:T(8,128)(2,1)}, u32[]{:S(2)}) copy-start(bf16[2688,16]{0,1:T(8,128)(2,1)} %param.18) | copy-start | bytes 258052
  7.9 7.3 %copy-start.5 = (bf16[2688,16]{0,1:T(8,128)(2,1)S(1)}, bf16[2688,16]{0,1:T(8,128)(2,1)}, u32[]{:S(2)}) copy-start(bf16[2688,16]{0,1:T(8,128)(2,1)} %param.16) | copy-start | bytes 258052
  8.0 19.2 %collective-permute-start.2 = (bf16[1024,512]{1,0:T(8,128)(2,1)S(1)}, bf16[1024,512]{1,0:T(8,128)(2,1)S(1)}, u32[]{:S(2)}, u32[]{:S(2)}) collective-permute-start(bf16[1024,512]{1,0:T(8,128)(2,1)S(1)} %pad_maximum_fusion.1), channel_id=1, source_target_pairs={{0,2},{2,4},{4,6},{6,8},{8,10},{10,12},{12,14},{14,16},{16,18},{18... | collective-permute-start | bytes 3145736 | tf_op jit(solution)/shard_map/ppermute | solution.py:353
  12.4 41.7 %collective-permute-start.3 = (bf16[1024,512]{1,0:T(8,128)(2,1)}, bf16[1024,512]{1,0:T(8,128)(2,1)}, u32[]{:S(2)}, u32[]{:S(2)}) collective-permute-start(bf16[1024,512]{1,0:T(8,128)(2,1)} %pad_maximum_fusion.2), channel_id=1, source_target_pairs={{0,2},{2,4},{4,6},{6,8},{8,10},{10,12},{12,14},{14,16},{16,18},{18... | collective-permute-start | bytes 3145736 | tf_op jit(solution)/shard_map/ppermute | solution.py:353
  16.4 7.5 %collective-permute-start = (f32[48,1024]{1,0:T(8,128)S(1)}, f32[48,1024]{1,0:T(8,128)S(1)}, u32[]{:S(2)}, u32[]{:S(2)}) collective-permute-start(f32[48,1024]{1,0:T(8,128)S(1)} %fusion), channel_id=1, source_target_pairs={{0,1},{1,0},{2,3},{3,2},{4,5},{5,4},{6,7},{7,6},{8,9},{9,8},{10,11... | collective-permute-start | bytes 589832 | tf_op jit(solution)/shard_map/ppermute | solution.py:358
  24.6 2.7 %collective-permute-start.1 = (f32[32,1024]{1,0:T(8,128)S(1)}, f32[32,1024]{1,0:T(8,128)S(1)}, u32[]{:S(2)}, u32[]{:S(2)}) collective-permute-start(f32[32,1024]{1,0:T(8,128)S(1)} %slice.97), channel_id=1, source_target_pairs={{0,2},{2,4},{4,6},{6,8},{8,10},{10,12},{12,14},{14,16},{16,18},{18... | collective-permute-start | bytes 393224 | tf_op jit(solution)/shard_map/ppermute | solution.py:353
  27.9 1.0 copy-start.15
  127.8 31.5 %collective-permute-start.5 = (bf16[32,1024]{1,0:T(8,128)(2,1)S(1)}, bf16[32,1024]{1,0:T(8,128)(2,1)S(1)}, u32[]{:S(2)}, u32[]{:S(2)}) collective-permute-start(bf16[32,1024]{1,0:T(8,128)(2,1)S(1)} %add_convert_fusion.3), channel_id=1, source_target_pairs={{2,0},{4,2},{6,4},{8,6},{10,8},{12,10},{14,12},{16,14},{18,16},{20... | collective-permute-start | bytes 196616 | tf_op jit(solution)/shard_map/ppermute | solution.py:353
  159.3 4.7 %collective-permute-start.6 = (bf16[48,1024]{1,0:T(8,128)(2,1)S(1)}, bf16[48,1024]{1,0:T(8,128)(2,1)S(1)}, u32[]{:S(2)}, u32[]{:S(2)}) collective-permute-start(bf16[48,1024]{1,0:T(8,128)(2,1)S(1)} %fusion.10), channel_id=1, source_target_pairs={{0,1},{1,0},{2,3},{3,2},{4,5},{5,4},{6,7},{7,6},{8,9},{9,8},{10,11... | collective-permute-start | bytes 294920 | tf_op jit(solution)/shard_map/ppermute | solution.py:358
  168.3 0.8 copy-start.8
  168.4 0.8 copy-start.9
  168.4 0.9 copy-start.6
  168.4 0.9 copy-start.13
  168.4 0.9 copy-start.14
  168.4 0.9 copy-start.10
  168.4 0.9 copy-start.11
  168.4 0.9 copy-start.12
  168.4 0.9 copy-start.7
  169.5 4.0 %collective-permute-start.7 = (bf16[16,6144]{1,0:T(8,128)(2,1)S(1)}, bf16[16,6144]{1,0:T(8,128)(2,1)S(1)}, u32[]{:S(2)}, u32[]{:S(2)}) collective-permute-start(bf16[16,6144]{1,0:T(8,128)(2,1)S(1)} %select_convert_fusion), channel_id=1, source_target_pairs={{0,2},{2,0},{4,6},{6,4},{8,10},{10,8},{12,14},{14,12},{16,18},{18,... | collective-permute-start | bytes 589832 | tf_op jit(solution)/shard_map/ppermute | solution.py:358
  173.5 5.5 %collective-permute-start.8 = (bf16[16,3072]{1,0:T(8,128)(2,1)S(1)}, bf16[16,3072]{1,0:T(8,128)(2,1)S(1)}, u32[]{:S(2)}, u32[]{:S(2)}) collective-permute-start(bf16[16,3072]{1,0:T(8,128)(2,1)S(1)} %select_convert_fusion.1), channel_id=1, source_target_pairs={{0,4},{2,6},{4,0},{6,2},{8,12},{10,14},{12,8},{14,10},{16,20},{18,... | collective-permute-start | bytes 294920 | tf_op jit(solution)/shard_map/ppermute | solution.py:358
  179.1 4.9 %collective-permute-start.9 = (bf16[16,3072]{1,0:T(8,128)(2,1)S(1)}, bf16[16,3072]{1,0:T(8,128)(2,1)S(1)}, u32[]{:S(2)}, u32[]{:S(2)}) collective-permute-start(bf16[16,3072]{1,0:T(8,128)(2,1)S(1)} %add_convert_fusion.2), channel_id=1, source_target_pairs={{0,8},{2,10},{4,12},{6,14},{8,0},{10,2},{12,4},{14,6},{16,24},{18,... | collective-permute-start | bytes 294920 | tf_op jit(solution)/shard_map/ppermute | solution.py:358
  184.0 5.7 %collective-permute-start.10 = (bf16[16,3072]{1,0:T(8,128)(2,1)S(1)}, bf16[16,3072]{1,0:T(8,128)(2,1)S(1)}, u32[]{:S(2)}, u32[]{:S(2)}) collective-permute-start(bf16[16,3072]{1,0:T(8,128)(2,1)S(1)} %add_convert_fusion.1), channel_id=1, source_target_pairs={{0,16},{2,18},{4,20},{6,22},{8,24},{10,26},{12,28},{14,30},{16,0},... | collective-permute-start | bytes 294920 | tf_op jit(solution)/shard_map/ppermute | solution.py:358
  189.8 4.7 %collective-permute-start.11 = (bf16[16,3072]{1,0:T(8,128)(2,1)S(1)}, bf16[16,3072]{1,0:T(8,128)(2,1)S(1)}, u32[]{:S(2)}, u32[]{:S(2)}) collective-permute-start(bf16[16,3072]{1,0:T(8,128)(2,1)S(1)} %add_convert_fusion), channel_id=1, source_target_pairs={{0,4},{2,6},{4,0},{6,2},{8,12},{10,14},{12,8},{14,10},{16,20},{18,... | collective-permute-start | bytes 294920 | tf_op jit(solution)/shard_map/ppermute | solution.py:358
  194.5 1.5 collective-permute-start.12
  (2 other events, 1.3 us)
where the time goes:
time: 199 us; the launch traced here: 198 us
  Pallas kernels  97.8 us (49%)
  waiting for transfers between devices  53 us (27%)
  starting transfers between devices  28.5 us (14%)
  local copies, waits for them, and re-layouts  6.23 us (3%)
  other arithmetic  6.14 us (3%)
  matrix products  5.42 us (3%)
    pallas_call x3, Pallas kernels, attention(): pl.pallas_call(functools.partial(attention_body, group, rank, rows), grid...  97.8 us
    ppermute x5, waiting for transfers between devices, shifted(): return lax.ppermute(shard, axis, pairs)  29.7 us
    ppermute x8, waiting for transfers between devices, exchanged(): return lax.ppermute(shard, axis, [(i, i ^ step) for i in range(length)])  23.3 us
    ppermute x8, starting transfers between devices, exchanged(): return lax.ppermute(shard, axis, [(i, i ^ step) for i in range(length)])  15.1 us
    ppermute x5, starting transfers between devices, shifted(): return lax.ppermute(shard, axis, pairs)  13.4 us
    dot_general x1, matrix products, layer(): lax.dot_general(parts, activations, (((1,), (1,)), ((), ())), preferred_e...  4.34 us
  transfers between devices with their start and end apart: 13, of which 10 were waited for; matrix products, arithmetic and copies ran while one was open for 2% of the time, Pallas kernels for 25%

commit v1 on v0

--- a/solution.py
+++ b/solution.py
@@ -52,7 +52,10 @@
     group,
     rank,
     rows,
+    fresh,
     bias_ref,
+    before_ref,
+    before_prior_ref,
     rank_ref,
     prior_rank_ref,
     fq_ref,
@@ -66,6 +69,7 @@
     uv_ref,
     inner_ref,
     inner_prior_ref,
+    prior_low_ref,
     upq_ref,
     upk_ref,
     upv_ref,
@@ -79,12 +83,13 @@
     s_scr,
     dp_scr,
     ds_scr,
+    e_scr,
 ):
     head = pl.program_id(0)
     own = fk_ref.shape[0]
     width = HEAD_WIDTH
     tiles = own // rows
-    half = rows // 2
+    half = rows
     lanes = group * rows
     scale = width**-0.5
     factor = scale * LOG2E
@@ -100,8 +105,12 @@
             ranks_t[at : at + rank, :own] = blank
             ranks_t[at + rank : at + 3 * rank, :own] = prior[part]
         ranks[...] = ranks_t[...].astype(F32).T.astype(BF16)
-        inner_ref[...] = jnp.zeros_like(inner_ref)
-        inner_prior_ref[...] = jnp.zeros_like(inner_prior_ref)
+        if fresh:
+            inner_ref[...] = jnp.zeros_like(inner_ref)
+            inner_prior_ref[...] = jnp.zeros_like(inner_prior_ref)
+        else:
+            inner_ref[...] = before_ref[...]
+            inner_prior_ref[...] = before_prior_ref[...]
 
     def stacked(up, kind):
         pieces = []
@@ -149,10 +158,6 @@
             axis=1,
         )
 
-    def tile_rows(block, tile):
-        start = (block + tile) * rows
-        return slice(start, start + rows)
-
     def tile_bias(block, tile):
         return bias if 0 < tile and block + tile < tiles else None
 
@@ -163,13 +168,15 @@
         q_t = across(lifted(fq_ref[here], lift))
         do_t = across(do_ref[here])
         highest = None
+        window = slice(block * rows, (block + tiles + 1) * rows)
+        all_scores = dot_nn(k_all[window], q_t)
+        all_grads = dot_nn(v_all[window], do_t)
         for tile in range(tiles):
-            scores = dot_nn(k_all[tile_rows(block, tile)], q_t)
-            grads = dot_nn(v_all[tile_rows(block, tile)], do_t)
+            scores = all_scores[tile * rows : (tile + 1) * rows]
+            grads = all_grads[tile * rows : (tile + 1) * rows]
             if tile == 0:
-                last = dot_nn(k_all[tile_rows(block, tiles)], q_t)
-                scores = jnp.where(earlier, scores + bias, last)
-                grads = jnp.where(earlier, grads, dot_nn(v_all[tile_rows(block, tiles)], do_t))
+                scores = jnp.where(earlier, scores + bias, all_scores[tiles * rows :])
+                grads = jnp.where(earlier, grads, all_grads[tiles * rows :])
             s_scr[slot, tile] = scores
             dp_scr[slot, tile] = grads
             high = fold8(scores, jnp.max)
@@ -201,13 +208,6 @@
             q_scaled=(state[block]["q_t"].astype(F32) * inverse).astype(BF16),
         )
 
-    def accumulate(acc, block, tile, value):
-        fresh = block == 0 or tile == tiles
-        if fresh:
-            acc[:, tile_rows(block, tile)] = value
-        else:
-            acc[:, tile_rows(block, tile)] += value
-
     def gradients(block):
         slot = block % 2
         now = state[block]
@@ -225,10 +225,17 @@
             for to, grad, exponent in parts:
                 grad_low = grad.astype(BF16)
                 ds_scr[slot, to * rows : (to + 1) * rows] = grad_low
-                accumulate(dk_acc, block, to, dot_nt(now["q_scaled"], grad_low))
-                accumulate(dv_acc, block, to, dot_nt(now["do_scaled"], exponent.astype(BF16)))
+                e_scr[slot, to * rows : (to + 1) * rows] = exponent.astype(BF16)
             yield True
         window = slice(block * rows, (block + tiles + 1) * rows)
+        for acc, left, right in ((dk_acc, now["q_scaled"], ds_scr), (dv_acc, now["do_scaled"], e_scr)):
+            value = dot_nt(left, right[slot])
+            if block:
+                edge = (block + tiles) * rows
+                acc[:, block * rows : edge] += value[:, : tiles * rows]
+                acc[:, edge : edge + rows] = value[:, tiles * rows :]
+            else:
+                acc[:, window] = value
         dq = dot_nn(k_t[:, window], ds_scr[slot]) * (now["inverse"] * scale)
         dq = dq.astype(BF16)
         up = uq_ref[...]
@@ -256,14 +263,11 @@
                 upq_ref[:, columns] += value
 
     alternate(products(0))
-    alternate(products(1), exponents(0))
     for block in range(tiles):
-        streams = [gradients(block)]
-        if block + 2 < tiles:
-            streams.append(products(block + 2))
+        alternate(exponents(block))
         if block + 1 < tiles:
-            streams.append(exponents(block + 1))
-        alternate(*streams)
+            alternate(products(block + 1))
+        alternate(gradients(block))
 
     for kind, acc, up_ref, out_ref, mult in (
         (1, dk_acc, uk_ref, upk_ref, scale),
@@ -274,9 +278,10 @@
         inner = dot_nn(up_ref[...], low)
         inner_prior_ref[(kind - 1) * rank : kind * rank, :] += inner[:, :own]
         inner_ref[kind * rank : (kind + 1) * rank, :] += inner[:, own:]
-
-
-def attention(first, heads, bias, rank_t, prior_rank_t, fq, do, fk, fv, packed, uq, uk, uv, rows=256):
+    prior_low_ref[...] = inner_prior_ref[...].astype(BF16)
+
+
+def attention(first, heads, bias, before, before_prior, rank_t, prior_rank_t, fq, do, fk, fv, packed, uq, uk, uv, rows=256):
     rank = uq.shape[0]
     own = fk.shape[0]
     width = HEAD_WIDTH
@@ -289,6 +294,8 @@
     chunk = lambda h: (0, h)
     in_specs = [
         pl.BlockSpec(memory_space=pltpu.SMEM),
+        pl.BlockSpec(before.shape, whole),
+        pl.BlockSpec(before_prior.shape, whole),
         pl.BlockSpec(rank_t.shape, whole),
         pl.BlockSpec(prior_rank_t.shape, whole),
         pl.BlockSpec((own, wide), key),
@@ -304,6 +311,7 @@
     out_specs = [
         pl.BlockSpec((3 * rank, own), whole),
         pl.BlockSpec((2 * rank, own), whole),
+        pl.BlockSpec((2 * rank, own), whole),
         pl.BlockSpec((rank, wide), chunk),
         pl.BlockSpec((rank, width), chunk),
         pl.BlockSpec((rank, width), chunk),
@@ -311,6 +319,7 @@
     out_shape = [
         jax.ShapeDtypeStruct((3 * rank, own), F32),
         jax.ShapeDtypeStruct((2 * rank, own), F32),
+        jax.ShapeDtypeStruct((2 * rank, own), BF16),
         jax.ShapeDtypeStruct((rank, heads * wide), F32),
         jax.ShapeDtypeStruct((rank, heads * width), F32),
         jax.ShapeDtypeStruct((rank, heads * width), F32),
@@ -326,10 +335,11 @@
         pltpu.VMEM((2, tiles, rows, lanes), F32),
         pltpu.VMEM((2, tiles, rows, lanes), F32),
         pltpu.VMEM((2, (tiles + 1) * rows, lanes), BF16),
+        pltpu.VMEM((2, (tiles + 1) * rows, lanes), BF16),
     ]
     pairs = heads * group * own * own
     return pl.pallas_call(
-        functools.partial(attention_body, group, rank, rows),
+        functools.partial(attention_body, group, rank, rows, first == 0),
         grid=(heads,),
         in_specs=in_specs,
         out_specs=out_specs,
@@ -344,7 +354,7 @@
             bytes_accessed=heads * own * width * (4 * group + 8),
         ),
         name="banded_attention",
-    )(bias, rank_t, prior_rank_t, fq, do, fk, packed, fv, packed, uq, uk, uv)
+    )(bias, before, before_prior, rank_t, prior_rank_t, fq, do, fk, packed, fv, packed, uq, uk, uv)
 
 
 def shifted(shard, axis, by):
@@ -431,13 +441,15 @@
         prior.append((first, count, shifted(packed, "ctx", 1)))
         first += count
     bias = jnp.where(lax.axis_index("ctx") == 0, NEGATIVE, 0.0).astype(F32).reshape(1)
-    inner = inner_prior = None
+    inner, inner_prior = rank_t, prior_rank_t
     ups = []
     for first, count, packed in prior:
-        one, one_prior, upq, upk, upv = attention(
+        inner, inner_prior, prior_low, upq, upk, upv = attention(
             first,
             count,
             bias,
+            inner,
+            inner_prior,
             rank_t,
             prior_rank_t,
             frozen_query_rows,
@@ -449,11 +461,9 @@
             key_up_weight,
             value_up_weight,
         )
-        inner = one if inner is None else inner + one
-        inner_prior = one_prior if inner_prior is None else inner_prior + one_prior
         ups.append((upq, upk, upv))
-    back = shifted(inner_prior.astype(BF16), "ctx", -1).astype(F32)
-    inner = jnp.concatenate([inner[:rank], inner[rank:] + back], axis=0)
+    back = shifted(prior_low, "ctx", -1).astype(F32)
+    inner = inner + jnp.pad(back, ((rank, 0), (0, 0)))
     inner = summed(inner, "heads", BF16)
     parts = jnp.concatenate(split2(inner), axis=0)
     down_parts = lax.dot_general(

time: 199 us -> 196 us (0.985)
  Pallas kernels: 97.8 us -> 94.4 us
    pallas_call x3, Pallas kernels: 97.8 us -> 94.4 us  [attention(): pl.pallas_call(functools.partial(attention_body, group, rank, rows, first...]
  transfers between devices with their start and end apart: 13 -> 13, of which waited for: 10 -> 10; matrix products, arithmetic and copies ran while one was open for 2% -> 1% of each run, Pallas kernels for 25% -> 25%
where the time goes in v1:
time: 196 us
  Pallas kernels  94.4 us (48%)
  waiting for transfers between devices  54.7 us (28%)
  starting transfers between devices  28.3 us (14%)
  local copies, waits for them, and re-layouts  6.23 us (3%)
  other arithmetic  5.79 us (3%)
  matrix products  5.42 us (3%)
    pallas_call x3, Pallas kernels, attention(): pl.pallas_call(functools.partial(attention_body, group, rank, rows, first...  94.4 us
    ppermute x5, waiting for transfers between devices, shifted(): return lax.ppermute(shard, axis, pairs)  31.3 us
    ppermute x8, waiting for transfers between devices, exchanged(): return lax.ppermute(shard, axis, [(i, i ^ step) for i in range(length)])  23.3 us
    ppermute x8, starting transfers between devices, exchanged(): return lax.ppermute(shard, axis, [(i, i ^ step) for i in range(length)])  15.2 us
    ppermute x5, starting transfers between devices, shifted(): return lax.ppermute(shard, axis, pairs)  13.1 us
    dot_general x1, matrix products, layer(): lax.dot_general(parts, activations, (((1,), (1,)), ((), ())), preferred_e...  4.33 us
  transfers between devices with their start and end apart: 13, of which 10 were waited for; matrix products, arithmetic and copies ran while one was open for 1% of the time, Pallas kernels for 25%

profile of v1, /device:TPU:0, one launch (start us, length us, event | category | flops | bytes accessed | tf_op | source)
XLA Modules:
  0.0 195.9 jit_solution(15795029388447235822)
XLA Ops:
  0.7 1.2 slice-done.2
  2.2 1.6 pad_maximum_fusion
  3.8 4.0 %collective-permute-start.4 = (bf16[1024,1024]{1,0:T(8,128)(2,1)}, bf16[1024,1024]{1,0:T(8,128)(2,1)}, u32[]{:S(2)}, u32[]{:S(2)}) collective-permute-start(bf16[1024,1024]{1,0:T(8,128)(2,1)} %pad_maximum_fusion), channel_id=1, source_target_pairs={{0,2},{2,4},{4,6},{6,8},{8,10},{10,12},{12,14},{14,16},{16,18},{18... | collective-permute-start | bytes 6291464 | tf_op jit(solution)/shard_map/ppermute | solution.py:363
  8.0 3.3 %collective-permute-start.2 = (bf16[1024,512]{1,0:T(8,128)(2,1)S(1)}, bf16[1024,512]{1,0:T(8,128)(2,1)S(1)}, u32[]{:S(2)}, u32[]{:S(2)}) collective-permute-start(bf16[1024,512]{1,0:T(8,128)(2,1)S(1)} %pad_maximum_fusion.1), channel_id=1, source_target_pairs={{0,2},{2,4},{4,6},{6,8},{8,10},{10,12},{12,14},{14,16},{16,18},{18... | collective-permute-start | bytes 3145736 | tf_op jit(solution)/shard_map/ppermute | solution.py:363
  11.3 1.1 pad_maximum_fusion.2
  12.4 2.9 %collective-permute-start.3 = (bf16[1024,512]{1,0:T(8,128)(2,1)}, bf16[1024,512]{1,0:T(8,128)(2,1)}, u32[]{:S(2)}, u32[]{:S(2)}) collective-permute-start(bf16[1024,512]{1,0:T(8,128)(2,1)} %pad_maximum_fusion.2), channel_id=1, source_target_pairs={{0,2},{2,4},{4,6},{6,8},{8,10},{10,12},{12,14},{14,16},{16,18},{18... | collective-permute-start | bytes 3145736 | tf_op jit(solution)/shard_map/ppermute | solution.py:363
  15.3 1.1 fusion
  16.4 1.6 collective-permute-start
  17.9 6.0 %collective-permute-done = f32[48,1024]{1,0:T(8,128)S(1)} collective-permute-done((f32[48,1024]{1,0:T(8,128)S(1)}, f32[48,1024]{1,0:T(8,128)S(1)}, u32[]{:S(2)}, u32[]{:S(2)}) %collective-permute-start) | collective-permute-done | bytes 196640 | tf_op jit(solution)/shard_map/ppermute | solution.py:368
  24.6 1.7 collective-permute-start.1
  26.3 1.0 collective-permute-done.1.before_prior_ref.prior_rank_ref
  27.9 1.0 copy-done.15
  28.9 24.5 %banded_attention.3 = (f32[48,1024]{1,0:T(8,128)}, f32[32,1024]{1,0:T(8,128)}, bf16[32,1024]{1,0:T(8,128)(2,1)}, f32[16,512]{1,0:T(8,128)}, f32[16,256]{1,0:T(8,128)}, /*index=5*/f32[16,256]{1,0:T(8,128)}) custom-call(f32[1]{0:T(128)} %bitcast.bias_ref, f32[48,1024]{1,0:T(8,128)} %copy-done.2, f32[32,1024]{1,0:T(8,128)} %copy-done.16, f32[48,1024]{1,0:T(8,128)} %copy-done.2, ...), custom_call_target="tpu_custom_call" | custom-call | flops 5368709120 | bytes 4194304 | tf_op jit(solution)/shard_map/banded_attention/pallas_call | solution.py:341
  53.4 24.4 %banded_attention.4 = (f32[48,1024]{1,0:T(8,128)}, f32[32,1024]{1,0:T(8,128)}, bf16[32,1024]{1,0:T(8,128)(2,1)}, f32[16,512]{1,0:T(8,128)}, f32[16,256]{1,0:T(8,128)}, /*index=5*/f32[16,256]{1,0:T(8,128)}) custom-call(f32[1]{0:T(128)} %bitcast.bias_ref, f32[48,1024]{1,0:T(8,128)} %get-tuple-element.21.before_ref, ...), custom_call_target="tpu_custom_call" | custom-call | flops 5368709120 | bytes 4194304 | tf_op jit(solution)/shard_map/banded_attention/pallas_call | solution.py:341
  77.8 45.5 %banded_attention.5 = (f32[48,1024]{1,0:T(8,128)}, f32[32,1024]{1,0:T(8,128)}, bf16[32,1024]{1,0:T(8,128)(2,1)}, f32[16,1024]{1,0:T(8,128)}, f32[16,512]{1,0:T(8,128)}, /*index=5*/f32[16,512]{1,0:T(8,128)}) custom-call(f32[1]{0:T(128)} %bitcast.bias_ref, f32[48,1024]{1,0:T(8,128)} %get-tuple-element.23.before_ref, ...), custom_call_target="tpu_custom_call" | custom-call | flops 10737418240 | bytes 8388608 | tf_op jit(solution)/shard_map/banded_attention/pallas_call | solution.py:341
  123.3 1.3 collective-permute-start.5
  124.6 30.4 %collective-permute-done.5 = bf16[32,1024]{1,0:T(8,128)(2,1)S(1)} collective-permute-done((bf16[32,1024]{1,0:T(8,128)(2,1)}, bf16[32,1024]{1,0:T(8,128)(2,1)S(1)}, u32[]{:S(2)}, u32[]{:S(2)}) %collective-permute-start.5) | collective-permute-done | bytes 65568 | tf_op jit(solution)/shard_map/ppermute | solution.py:363
  156.0 1.6 collective-permute-start.6
  157.5 3.1 %collective-permute-done.6 = bf16[48,1024]{1,0:T(8,128)(2,1)S(1)} collective-permute-done((bf16[48,1024]{1,0:T(8,128)(2,1)S(1)}, bf16[48,1024]{1,0:T(8,128)(2,1)S(1)}, u32[]{:S(2)}, u32[]{:S(2)}) %collective-permute-start.6) | collective-permute-done | bytes 98336 | tf_op jit(solution)/shard_map/ppermute | solution.py:368
  160.7 1.0 fusion.11
  161.6 4.3 %fusion.6 = f32[96,2688]{1,0:T(8,128)S(1)} fusion(bf16[2688,1024]{1,0:T(8,128)(2,1)} %param.11, bf16[48,1024]{1,0:T(8,128)(2,1)S(1)} %get-tuple-element.48, bf16[48,1024]{1,0:T(8,128)(2,1)S(1)} %get-tuple-element.47), kind=kOutput, calls=%fused_computation.15 | convolution fusion | flops 528875520 | bytes 6733824 | tf_op jit(solution)/shard_map/dot_general | solution.py:469
  167.1 2.6 %collective-permute-start.7 = (bf16[16,6144]{1,0:T(8,128)(2,1)S(1)}, bf16[16,6144]{1,0:T(8,128)(2,1)S(1)}, u32[]{:S(2)}, u32[]{:S(2)}) collective-permute-start(bf16[16,6144]{1,0:T(8,128)(2,1)S(1)} %select_convert_fusion), channel_id=1, source_target_pairs={{0,2},{2,0},{4,6},{6,4},{8,10},{10,8},{12,14},{14,12},{16,18},{18,... | collective-permute-start | bytes 589832 | tf_op jit(solution)/shard_map/ppermute | solution.py:368
  169.7 1.1 collective-permute-done.7
  170.9 2.5 %collective-permute-start.8 = (bf16[16,3072]{1,0:T(8,128)(2,1)S(1)}, bf16[16,3072]{1,0:T(8,128)(2,1)S(1)}, u32[]{:S(2)}, u32[]{:S(2)}) collective-permute-start(bf16[16,3072]{1,0:T(8,128)(2,1)S(1)} %select_convert_fusion.1), channel_id=1, source_target_pairs={{0,4},{2,6},{4,0},{6,2},{8,12},{10,14},{12,8},{14,10},{16,20},{18,... | collective-permute-start | bytes 294920 | tf_op jit(solution)/shard_map/ppermute | solution.py:368
  173.3 3.3 %collective-permute-done.8 = bf16[16,3072]{1,0:T(8,128)(2,1)S(1)} collective-permute-done((bf16[16,3072]{1,0:T(8,128)(2,1)S(1)}, bf16[16,3072]{1,0:T(8,128)(2,1)S(1)}, u32[]{:S(2)}, u32[]{:S(2)}) %collective-permute-start.8) | collective-permute-done | bytes 98336 | tf_op jit(solution)/shard_map/ppermute | solution.py:368
  176.7 2.3 %collective-permute-start.9 = (bf16[16,3072]{1,0:T(8,128)(2,1)S(1)}, bf16[16,3072]{1,0:T(8,128)(2,1)S(1)}, u32[]{:S(2)}, u32[]{:S(2)}) collective-permute-start(bf16[16,3072]{1,0:T(8,128)(2,1)S(1)} %add_convert_fusion.2), channel_id=1, source_target_pairs={{0,8},{2,10},{4,12},{6,14},{8,0},{10,2},{12,4},{14,6},{16,24},{18,... | collective-permute-start | bytes 294920 | tf_op jit(solution)/shard_map/ppermute | solution.py:368
  179.0 2.6 %collective-permute-done.9 = bf16[16,3072]{1,0:T(8,128)(2,1)S(1)} collective-permute-done((bf16[16,3072]{1,0:T(8,128)(2,1)S(1)}, bf16[16,3072]{1,0:T(8,128)(2,1)S(1)}, u32[]{:S(2)}, u32[]{:S(2)}) %collective-permute-start.9) | collective-permute-done | bytes 98336 | tf_op jit(solution)/shard_map/ppermute | solution.py:368
  181.7 3.1 %collective-permute-start.10 = (bf16[16,3072]{1,0:T(8,128)(2,1)S(1)}, bf16[16,3072]{1,0:T(8,128)(2,1)S(1)}, u32[]{:S(2)}, u32[]{:S(2)}) collective-permute-start(bf16[16,3072]{1,0:T(8,128)(2,1)S(1)} %add_convert_fusion.1), channel_id=1, source_target_pairs={{0,16},{2,18},{4,20},{6,22},{8,24},{10,26},{12,28},{14,30},{16,0},... | collective-permute-start | bytes 294920 | tf_op jit(solution)/shard_map/ppermute | solution.py:368
  184.8 2.6 %collective-permute-done.10 = bf16[16,3072]{1,0:T(8,128)(2,1)S(1)} collective-permute-done((bf16[16,3072]{1,0:T(8,128)(2,1)S(1)}, bf16[16,3072]{1,0:T(8,128)(2,1)S(1)}, u32[]{:S(2)}, u32[]{:S(2)}) %collective-permute-start.10) | collective-permute-done | bytes 98336 | tf_op jit(solution)/shard_map/ppermute | solution.py:368
  187.4 1.5 collective-permute-start.11
  188.8 3.2 %collective-permute-done.11 = bf16[16,3072]{1,0:T(8,128)(2,1)S(1)} collective-permute-done((bf16[16,3072]{1,0:T(8,128)(2,1)S(1)}, bf16[16,3072]{1,0:T(8,128)(2,1)S(1)}, u32[]{:S(2)}, u32[]{:S(2)}) %collective-permute-start.11) | collective-permute-done | bytes 98336 | tf_op jit(solution)/shard_map/ppermute | solution.py:368
  192.2 1.4 collective-permute-done.12
  (77 shorter events, 6.3 us)
Async XLA Ops:
  0.6 1.2 slice-start.2
  0.6 1.5 slice-start.3
  0.7 7.1 %copy-start.1 = (bf16[1024,1024]{1,0:T(8,128)(2,1)S(1)}, bf16[1024,1024]{1,0:T(8,128)(2,1)}, u32[]{:S(2)}) copy-start(bf16[1024,1024]{1,0:T(8,128)(2,1)} %fv_ref.5) | copy-start | bytes 6291460
  2.2 5.6 %copy-start = (bf16[1024,1024]{1,0:T(8,128)(2,1)S(1)}, bf16[1024,1024]{1,0:T(8,128)(2,1)}, u32[]{:S(2)}) copy-start(bf16[1024,1024]{1,0:T(8,128)(2,1)} %fk_ref.5) | copy-start | bytes 6291460
  2.2 13.1 %slice-start = ((s8[5505024]{0:T(1024)(128)(4,1)}), s8[1310720]{0:T(1024)(128)(4,1)S(1)}, s32[]{:S(2)}) async-start(s8[5505024]{0:T(1024)(128)(4,1)} %bitcast.9), calls=%async_computation | async-start | bytes 2621440
  3.8 11.5 %slice-start.1 = ((s8[5505024]{0:T(1024)(128)(4,1)}), s8[4194304]{0:T(1024)(128)(4,1)S(1)}, s32[]{:S(2)}) async-start(s8[5505024]{0:T(1024)(128)(4,1)} %bitcast.9), calls=%async_computation.1 | async-start | bytes 8388608
  3.8 74.0 %collective-permute-start.4 = (bf16[1024,1024]{1,0:T(8,128)(2,1)}, bf16[1024,1024]{1,0:T(8,128)(2,1)}, u32[]{:S(2)}, u32[]{:S(2)}) collective-permute-start(bf16[1024,1024]{1,0:T(8,128)(2,1)} %pad_maximum_fusion), channel_id=1, source_target_pairs={{0,2},{2,4},{4,6},{6,8},{8,10},{10,12},{12,14},{14,16},{16,18},{18... | collective-permute-start | bytes 6291464 | tf_op jit(solution)/shard_map/ppermute | solution.py:363
  7.9 7.3 %copy-start.3 = (bf16[2688,16]{0,1:T(8,128)(2,1)S(1)}, bf16[2688,16]{0,1:T(8,128)(2,1)}, u32[]{:S(2)}) copy-start(bf16[2688,16]{0,1:T(8,128)(2,1)} %param.20) | copy-start | bytes 258052
  7.9 7.3 %copy-start.4 = (bf16[2688,16]{0,1:T(8,128)(2,1)S(1)}, bf16[2688,16]{0,1:T(8,128)(2,1)}, u32[]{:S(2)}) copy-start(bf16[2688,16]{0,1:T(8,128)(2,1)} %param.18) | copy-start | bytes 258052
  7.9 7.3 %copy-start.5 = (bf16[2688,16]{0,1:T(8,128)(2,1)S(1)}, bf16[2688,16]{0,1:T(8,128)(2,1)}, u32[]{:S(2)}) copy-start(bf16[2688,16]{0,1:T(8,128)(2,1)} %param.16) | copy-start | bytes 258052
  8.0 19.2 %collective-permute-start.2 = (bf16[1024,512]{1,0:T(8,128)(2,1)S(1)}, bf16[1024,512]{1,0:T(8,128)(2,1)S(1)}, u32[]{:S(2)}, u32[]{:S(2)}) collective-permute-start(bf16[1024,512]{1,0:T(8,128)(2,1)S(1)} %pad_maximum_fusion.1), channel_id=1, source_target_pairs={{0,2},{2,4},{4,6},{6,8},{8,10},{10,12},{12,14},{14,16},{16,18},{18... | collective-permute-start | bytes 3145736 | tf_op jit(solution)/shard_map/ppermute | solution.py:363
  12.4 41.0 %collective-permute-start.3 = (bf16[1024,512]{1,0:T(8,128)(2,1)}, bf16[1024,512]{1,0:T(8,128)(2,1)}, u32[]{:S(2)}, u32[]{:S(2)}) collective-permute-start(bf16[1024,512]{1,0:T(8,128)(2,1)} %pad_maximum_fusion.2), channel_id=1, source_target_pairs={{0,2},{2,4},{4,6},{6,8},{8,10},{10,12},{12,14},{14,16},{16,18},{18... | collective-permute-start | bytes 3145736 | tf_op jit(solution)/shard_map/ppermute | solution.py:363
  16.4 7.5 %collective-permute-start = (f32[48,1024]{1,0:T(8,128)S(1)}, f32[48,1024]{1,0:T(8,128)S(1)}, u32[]{:S(2)}, u32[]{:S(2)}) collective-permute-start(f32[48,1024]{1,0:T(8,128)S(1)} %fusion), channel_id=1, source_target_pairs={{0,1},{1,0},{2,3},{3,2},{4,5},{5,4},{6,7},{7,6},{8,9},{9,8},{10,11... | collective-permute-start | bytes 589832 | tf_op jit(solution)/shard_map/ppermute | solution.py:368
  24.6 2.7 %collective-permute-start.1 = (f32[32,1024]{1,0:T(8,128)S(1)}, f32[32,1024]{1,0:T(8,128)S(1)}, u32[]{:S(2)}, u32[]{:S(2)}) collective-permute-start(f32[32,1024]{1,0:T(8,128)S(1)} %slice.89), channel_id=1, source_target_pairs={{0,2},{2,4},{4,6},{6,8},{8,10},{10,12},{12,14},{14,16},{16,18},{18... | collective-permute-start | bytes 393224 | tf_op jit(solution)/shard_map/ppermute | solution.py:363
  27.9 1.0 copy-start.15
  123.3 31.7 %collective-permute-start.5 = (bf16[32,1024]{1,0:T(8,128)(2,1)}, bf16[32,1024]{1,0:T(8,128)(2,1)S(1)}, u32[]{:S(2)}, u32[]{:S(2)}) collective-permute-start(bf16[32,1024]{1,0:T(8,128)(2,1)} %get-tuple-element.26), channel_id=1, source_target_pairs={{2,0},{4,2},{6,4},{8,6},{10,8},{12,10},{14,12},{16,14},{18,16},{20... | collective-permute-start | bytes 196616 | tf_op jit(solution)/shard_map/ppermute | solution.py:363
  156.0 4.7 %collective-permute-start.6 = (bf16[48,1024]{1,0:T(8,128)(2,1)S(1)}, bf16[48,1024]{1,0:T(8,128)(2,1)S(1)}, u32[]{:S(2)}, u32[]{:S(2)}) collective-permute-start(bf16[48,1024]{1,0:T(8,128)(2,1)S(1)} %fusion.10), channel_id=1, source_target_pairs={{0,1},{1,0},{2,3},{3,2},{4,5},{5,4},{6,7},{7,6},{8,9},{9,8},{10,11... | collective-permute-start | bytes 294920 | tf_op jit(solution)/shard_map/ppermute | solution.py:368
  166.0 0.8 copy-start.7
  166.0 0.8 copy-start.9
  166.0 0.9 copy-start.6
  166.0 0.9 copy-start.12
  166.0 0.9 copy-start.14
  166.0 0.9 copy-start.10
  166.0 0.9 copy-start.11
  166.0 0.9 copy-start.13
  166.0 0.9 copy-start.8
  167.1 3.7 %collective-permute-start.7 = (bf16[16,6144]{1,0:T(8,128)(2,1)S(1)}, bf16[16,6144]{1,0:T(8,128)(2,1)S(1)}, u32[]{:S(2)}, u32[]{:S(2)}) collective-permute-start(bf16[16,6144]{1,0:T(8,128)(2,1)S(1)} %select_convert_fusion), channel_id=1, source_target_pairs={{0,2},{2,0},{4,6},{6,4},{8,10},{10,8},{12,14},{14,12},{16,18},{18,... | collective-permute-start | bytes 589832 | tf_op jit(solution)/shard_map/ppermute | solution.py:368
  170.9 5.8 %collective-permute-start.8 = (bf16[16,3072]{1,0:T(8,128)(2,1)S(1)}, bf16[16,3072]{1,0:T(8,128)(2,1)S(1)}, u32[]{:S(2)}, u32[]{:S(2)}) collective-permute-start(bf16[16,3072]{1,0:T(8,128)(2,1)S(1)} %select_convert_fusion.1), channel_id=1, source_target_pairs={{0,4},{2,6},{4,0},{6,2},{8,12},{10,14},{12,8},{14,10},{16,20},{18,... | collective-permute-start | bytes 294920 | tf_op jit(solution)/shard_map/ppermute | solution.py:368
  176.7 4.9 %collective-permute-start.9 = (bf16[16,3072]{1,0:T(8,128)(2,1)S(1)}, bf16[16,3072]{1,0:T(8,128)(2,1)S(1)}, u32[]{:S(2)}, u32[]{:S(2)}) collective-permute-start(bf16[16,3072]{1,0:T(8,128)(2,1)S(1)} %add_convert_fusion.2), channel_id=1, source_target_pairs={{0,8},{2,10},{4,12},{6,14},{8,0},{10,2},{12,4},{14,6},{16,24},{18,... | collective-permute-start | bytes 294920 | tf_op jit(solution)/shard_map/ppermute | solution.py:368
  181.7 5.7 %collective-permute-start.10 = (bf16[16,3072]{1,0:T(8,128)(2,1)S(1)}, bf16[16,3072]{1,0:T(8,128)(2,1)S(1)}, u32[]{:S(2)}, u32[]{:S(2)}) collective-permute-start(bf16[16,3072]{1,0:T(8,128)(2,1)S(1)} %add_convert_fusion.1), channel_id=1, source_target_pairs={{0,16},{2,18},{4,20},{6,22},{8,24},{10,26},{12,28},{14,30},{16,0},... | collective-permute-start | bytes 294920 | tf_op jit(solution)/shard_map/ppermute | solution.py:368
  187.4 4.7 %collective-permute-start.11 = (bf16[16,3072]{1,0:T(8,128)(2,1)S(1)}, bf16[16,3072]{1,0:T(8,128)(2,1)S(1)}, u32[]{:S(2)}, u32[]{:S(2)}) collective-permute-start(bf16[16,3072]{1,0:T(8,128)(2,1)S(1)} %add_convert_fusion), channel_id=1, source_target_pairs={{0,4},{2,6},{4,0},{6,2},{8,12},{10,14},{12,8},{14,10},{16,20},{18,... | collective-permute-start | bytes 294920 | tf_op jit(solution)/shard_map/ppermute | solution.py:368
  192.1 1.5 collective-permute-start.12
  (2 other events, 1.3 us)

commit v2 on v1

--- a/solution.py
+++ b/solution.py
@@ -14,11 +14,6 @@
 LOG2E = 1.4426950408889634
 F32 = jnp.float32
 BF16 = jnp.bfloat16
-
-
-def split2(x):
-    high = x.astype(BF16)
-    return high, (x - high.astype(F32)).astype(BF16)
 
 
 def split3(x):
@@ -465,11 +460,9 @@
     back = shifted(prior_low, "ctx", -1).astype(F32)
     inner = inner + jnp.pad(back, ((rank, 0), (0, 0)))
     inner = summed(inner, "heads", BF16)
-    parts = jnp.concatenate(split2(inner), axis=0)
-    down_parts = lax.dot_general(
-        parts, activations, (((1,), (1,)), ((), ())), preferred_element_type=F32
-    )
-    down_t = down_parts[: 3 * rank] + down_parts[3 * rank :]
+    down_t = lax.dot_general(
+        activations, inner.astype(BF16), (((1,), (1,)), ((), ())), preferred_element_type=F32
+    ).T
     pieces = [down_t[kind * rank : (kind + 1) * rank] for kind in range(3)]
     pieces += [jnp.concatenate([up[kind] for up in ups], axis=1) for kind in range(3)]
     packed = ADAPTER_SCALE * jnp.concatenate(pieces, axis=1)

time: 196 us -> 195 us (level)
  no operation moved by 1% of the time
where the time goes in v2:
time: 195 us; the launch traced here: 194 us
  Pallas kernels  94.4 us (48%)
  waiting for transfers between devices  54.6 us (28%)
  starting transfers between devices  28.3 us (15%)
  local copies, waits for them, and re-layouts  5.59 us (3%)
  matrix products  5.49 us (3%)
  other arithmetic  4.78 us (2%)
    pallas_call x3, Pallas kernels, attention(): pl.pallas_call(functools.partial(attention_body, group, rank, rows, first...  94.4 us
    ppermute x5, waiting for transfers between devices, shifted(): return lax.ppermute(shard, axis, pairs)  31.3 us
    ppermute x8, waiting for transfers between devices, exchanged(): return lax.ppermute(shard, axis, [(i, i ^ step) for i in range(length)])  23.3 us
    ppermute x8, starting transfers between devices, exchanged(): return lax.ppermute(shard, axis, [(i, i ^ step) for i in range(length)])  15.1 us
    ppermute x5, starting transfers between devices, shifted(): return lax.ppermute(shard, axis, pairs)  13.1 us
    dot_general x1, matrix products, layer(): lax.dot_general(activations, inner.astype(BF16), (((1,), (1,)), ((), ()))...  4.41 us
  transfers between devices with their start and end apart: 13, of which 10 were waited for; matrix products, arithmetic and copies ran while one was open for 1% of the time, Pallas kernels for 25%

profile of v2, /device:TPU:0, one launch (start us, length us, event | category | flops | bytes accessed | tf_op | source)
XLA Modules:
  0.0 194.3 jit_solution(6109389145064477168)
XLA Ops:
  0.7 1.2 slice-done.2
  2.2 1.6 pad_maximum_fusion
  3.8 4.0 %collective-permute-start.4 = (bf16[1024,1024]{1,0:T(8,128)(2,1)}, bf16[1024,1024]{1,0:T(8,128)(2,1)}, u32[]{:S(2)}, u32[]{:S(2)}) collective-permute-start(bf16[1024,1024]{1,0:T(8,128)(2,1)} %pad_maximum_fusion), channel_id=1, source_target_pairs={{0,2},{2,4},{4,6},{6,8},{8,10},{10,12},{12,14},{14,16},{16,18},{18... | collective-permute-start | bytes 6291464 | tf_op jit(solution)/shard_map/ppermute | solution.py:358
  8.1 3.3 %collective-permute-start.2 = (bf16[1024,512]{1,0:T(8,128)(2,1)S(1)}, bf16[1024,512]{1,0:T(8,128)(2,1)S(1)}, u32[]{:S(2)}, u32[]{:S(2)}) collective-permute-start(bf16[1024,512]{1,0:T(8,128)(2,1)S(1)} %pad_maximum_fusion.1), channel_id=1, source_target_pairs={{0,2},{2,4},{4,6},{6,8},{8,10},{10,12},{12,14},{14,16},{16,18},{18... | collective-permute-start | bytes 3145736 | tf_op jit(solution)/shard_map/ppermute | solution.py:358
  11.3 1.1 pad_maximum_fusion.2
  12.4 2.8 %collective-permute-start.3 = (bf16[1024,512]{1,0:T(8,128)(2,1)}, bf16[1024,512]{1,0:T(8,128)(2,1)}, u32[]{:S(2)}, u32[]{:S(2)}) collective-permute-start(bf16[1024,512]{1,0:T(8,128)(2,1)} %pad_maximum_fusion.2), channel_id=1, source_target_pairs={{0,2},{2,4},{4,6},{6,8},{8,10},{10,12},{12,14},{14,16},{16,18},{18... | collective-permute-start | bytes 3145736 | tf_op jit(solution)/shard_map/ppermute | solution.py:358
  15.3 1.1 fusion
  16.4 1.6 collective-permute-start
  17.9 6.0 %collective-permute-done = f32[48,1024]{1,0:T(8,128)S(1)} collective-permute-done((f32[48,1024]{1,0:T(8,128)S(1)}, f32[48,1024]{1,0:T(8,128)S(1)}, u32[]{:S(2)}, u32[]{:S(2)}) %collective-permute-start) | collective-permute-done | bytes 196640 | tf_op jit(solution)/shard_map/ppermute | solution.py:363
  24.6 1.7 collective-permute-start.1
  26.3 1.0 collective-permute-done.1.before_prior_ref.prior_rank_ref
  27.9 1.0 copy-done.15
  28.9 24.5 %banded_attention.3 = (f32[48,1024]{1,0:T(8,128)}, f32[32,1024]{1,0:T(8,128)}, bf16[32,1024]{1,0:T(8,128)(2,1)}, f32[16,512]{1,0:T(8,128)}, f32[16,256]{1,0:T(8,128)}, /*index=5*/f32[16,256]{1,0:T(8,128)}) custom-call(f32[1]{0:T(128)} %bitcast.bias_ref, f32[48,1024]{1,0:T(8,128)} %copy-done.2, f32[32,1024]{1,0:T(8,128)} %copy-done.16, f32[48,1024]{1,0:T(8,128)} %copy-done.2, ...), custom_call_target="tpu_custom_call" | custom-call | flops 5368709120 | bytes 4194304 | tf_op jit(solution)/shard_map/banded_attention/pallas_call | solution.py:336
  53.5 24.4 %banded_attention.4 = (f32[48,1024]{1,0:T(8,128)}, f32[32,1024]{1,0:T(8,128)}, bf16[32,1024]{1,0:T(8,128)(2,1)}, f32[16,512]{1,0:T(8,128)}, f32[16,256]{1,0:T(8,128)}, /*index=5*/f32[16,256]{1,0:T(8,128)}) custom-call(f32[1]{0:T(128)} %bitcast.bias_ref, f32[48,1024]{1,0:T(8,128)} %get-tuple-element.21.before_ref, ...), custom_call_target="tpu_custom_call" | custom-call | flops 5368709120 | bytes 4194304 | tf_op jit(solution)/shard_map/banded_attention/pallas_call | solution.py:336
  77.9 45.5 %banded_attention.5 = (f32[48,1024]{1,0:T(8,128)}, f32[32,1024]{1,0:T(8,128)}, bf16[32,1024]{1,0:T(8,128)(2,1)}, f32[16,1024]{1,0:T(8,128)}, f32[16,512]{1,0:T(8,128)}, /*index=5*/f32[16,512]{1,0:T(8,128)}) custom-call(f32[1]{0:T(128)} %bitcast.bias_ref, f32[48,1024]{1,0:T(8,128)} %get-tuple-element.23.before_ref, ...), custom_call_target="tpu_custom_call" | custom-call | flops 10737418240 | bytes 8388608 | tf_op jit(solution)/shard_map/banded_attention/pallas_call | solution.py:336
  123.4 1.3 collective-permute-start.5
  124.7 30.4 %collective-permute-done.5 = bf16[32,1024]{1,0:T(8,128)(2,1)S(1)} collective-permute-done((bf16[32,1024]{1,0:T(8,128)(2,1)}, bf16[32,1024]{1,0:T(8,128)(2,1)S(1)}, u32[]{:S(2)}, u32[]{:S(2)}) %collective-permute-start.5) | collective-permute-done | bytes 65568 | tf_op jit(solution)/shard_map/ppermute | solution.py:358
  155.1 0.9 fusion.6
  156.0 1.6 collective-permute-start.6
  157.6 3.1 %collective-permute-done.6 = bf16[48,1024]{1,0:T(8,128)(2,1)S(1)} collective-permute-done((bf16[48,1024]{1,0:T(8,128)(2,1)S(1)}, bf16[48,1024]{1,0:T(8,128)(2,1)S(1)}, u32[]{:S(2)}, u32[]{:S(2)}) %collective-permute-start.6) | collective-permute-done | bytes 98336 | tf_op jit(solution)/shard_map/ppermute | solution.py:363
  160.7 4.4 %fusion.7 = f32[48,2688]{1,0:T(8,128)S(1)} fusion(bf16[2688,1024]{1,0:T(8,128)(2,1)} %param.11, bf16[48,1024]{1,0:T(8,128)(2,1)S(1)} %collective-permute-done.6, f32[48,1024]{1,0:T(8,128)} %get-tuple-element.25, bf16[32,1024]{1,0:T(8,128)(2,1)S(1)} %collective-permute-done.5), kind=kOutput, calls=%fused_computation.30 | convolution fusion | flops 264486912 | bytes 6381568 | tf_op jit(solution)/shard_map/dot_general | solution.py:463
  165.5 2.6 %collective-permute-start.7 = (bf16[16,6144]{1,0:T(8,128)(2,1)S(1)}, bf16[16,6144]{1,0:T(8,128)(2,1)S(1)}, u32[]{:S(2)}, u32[]{:S(2)}) collective-permute-start(bf16[16,6144]{1,0:T(8,128)(2,1)S(1)} %select_convert_fusion), channel_id=1, source_target_pairs={{0,2},{2,0},{4,6},{6,4},{8,10},{10,8},{12,14},{14,12},{16,18},{18,... | collective-permute-start | bytes 589832 | tf_op jit(solution)/shard_map/ppermute | solution.py:363
  168.1 1.1 collective-permute-done.7
  169.3 2.5 %collective-permute-start.8 = (bf16[16,3072]{1,0:T(8,128)(2,1)S(1)}, bf16[16,3072]{1,0:T(8,128)(2,1)S(1)}, u32[]{:S(2)}, u32[]{:S(2)}) collective-permute-start(bf16[16,3072]{1,0:T(8,128)(2,1)S(1)} %select_convert_fusion.1), channel_id=1, source_target_pairs={{0,4},{2,6},{4,0},{6,2},{8,12},{10,14},{12,8},{14,10},{16,20},{18,... | collective-permute-start | bytes 294920 | tf_op jit(solution)/shard_map/ppermute | solution.py:363
  171.7 3.3 %collective-permute-done.8 = bf16[16,3072]{1,0:T(8,128)(2,1)S(1)} collective-permute-done((bf16[16,3072]{1,0:T(8,128)(2,1)S(1)}, bf16[16,3072]{1,0:T(8,128)(2,1)S(1)}, u32[]{:S(2)}, u32[]{:S(2)}) %collective-permute-start.8) | collective-permute-done | bytes 98336 | tf_op jit(solution)/shard_map/ppermute | solution.py:363
  175.1 2.3 %collective-permute-start.9 = (bf16[16,3072]{1,0:T(8,128)(2,1)S(1)}, bf16[16,3072]{1,0:T(8,128)(2,1)S(1)}, u32[]{:S(2)}, u32[]{:S(2)}) collective-permute-start(bf16[16,3072]{1,0:T(8,128)(2,1)S(1)} %add_convert_fusion.2), channel_id=1, source_target_pairs={{0,8},{2,10},{4,12},{6,14},{8,0},{10,2},{12,4},{14,6},{16,24},{18,... | collective-permute-start | bytes 294920 | tf_op jit(solution)/shard_map/ppermute | solution.py:363
  177.4 2.6 %collective-permute-done.9 = bf16[16,3072]{1,0:T(8,128)(2,1)S(1)} collective-permute-done((bf16[16,3072]{1,0:T(8,128)(2,1)S(1)}, bf16[16,3072]{1,0:T(8,128)(2,1)S(1)}, u32[]{:S(2)}, u32[]{:S(2)}) %collective-permute-start.9) | collective-permute-done | bytes 98336 | tf_op jit(solution)/shard_map/ppermute | solution.py:363
  180.1 3.1 %collective-permute-start.10 = (bf16[16,3072]{1,0:T(8,128)(2,1)S(1)}, bf16[16,3072]{1,0:T(8,128)(2,1)S(1)}, u32[]{:S(2)}, u32[]{:S(2)}) collective-permute-start(bf16[16,3072]{1,0:T(8,128)(2,1)S(1)} %add_convert_fusion.1), channel_id=1, source_target_pairs={{0,16},{2,18},{4,20},{6,22},{8,24},{10,26},{12,28},{14,30},{16,0},... | collective-permute-start | bytes 294920 | tf_op jit(solution)/shard_map/ppermute | solution.py:363
  183.2 2.6 %collective-permute-done.10 = bf16[16,3072]{1,0:T(8,128)(2,1)S(1)} collective-permute-done((bf16[16,3072]{1,0:T(8,128)(2,1)S(1)}, bf16[16,3072]{1,0:T(8,128)(2,1)S(1)}, u32[]{:S(2)}, u32[]{:S(2)}) %collective-permute-start.10) | collective-permute-done | bytes 98336 | tf_op jit(solution)/shard_map/ppermute | solution.py:363
  185.8 1.5 collective-permute-start.11
  187.2 3.2 %collective-permute-done.11 = bf16[16,3072]{1,0:T(8,128)(2,1)S(1)} collective-permute-done((bf16[16,3072]{1,0:T(8,128)(2,1)S(1)}, bf16[16,3072]{1,0:T(8,128)(2,1)S(1)}, u32[]{:S(2)}, u32[]{:S(2)}) %collective-permute-start.11) | collective-permute-done | bytes 98336 | tf_op jit(solution)/shard_map/ppermute | solution.py:363
  190.6 1.4 collective-permute-done.12
  (75 shorter events, 4.7 us)
Async XLA Ops:
  0.6 1.2 slice-start.2
  0.6 1.5 slice-start.3
  0.7 7.1 %copy-start.1 = (bf16[1024,1024]{1,0:T(8,128)(2,1)S(1)}, bf16[1024,1024]{1,0:T(8,128)(2,1)}, u32[]{:S(2)}) copy-start(bf16[1024,1024]{1,0:T(8,128)(2,1)} %fv_ref.5) | copy-start | bytes 6291460
  2.2 5.6 %copy-start = (bf16[1024,1024]{1,0:T(8,128)(2,1)S(1)}, bf16[1024,1024]{1,0:T(8,128)(2,1)}, u32[]{:S(2)}) copy-start(bf16[1024,1024]{1,0:T(8,128)(2,1)} %fk_ref.5) | copy-start | bytes 6291460
  2.2 13.1 %slice-start = ((s8[5505024]{0:T(1024)(128)(4,1)}), s8[1310720]{0:T(1024)(128)(4,1)S(1)}, s32[]{:S(2)}) async-start(s8[5505024]{0:T(1024)(128)(4,1)} %bitcast.9), calls=%async_computation | async-start | bytes 2621440
  3.8 11.5 %slice-start.1 = ((s8[5505024]{0:T(1024)(128)(4,1)}), s8[4194304]{0:T(1024)(128)(4,1)S(1)}, s32[]{:S(2)}) async-start(s8[5505024]{0:T(1024)(128)(4,1)} %bitcast.9), calls=%async_computation.1 | async-start | bytes 8388608
  3.8 74.1 %collective-permute-start.4 = (bf16[1024,1024]{1,0:T(8,128)(2,1)}, bf16[1024,1024]{1,0:T(8,128)(2,1)}, u32[]{:S(2)}, u32[]{:S(2)}) collective-permute-start(bf16[1024,1024]{1,0:T(8,128)(2,1)} %pad_maximum_fusion), channel_id=1, source_target_pairs={{0,2},{2,4},{4,6},{6,8},{8,10},{10,12},{12,14},{14,16},{16,18},{18... | collective-permute-start | bytes 6291464 | tf_op jit(solution)/shard_map/ppermute | solution.py:358
  7.9 7.3 %copy-start.3 = (bf16[2688,16]{0,1:T(8,128)(2,1)S(1)}, bf16[2688,16]{0,1:T(8,128)(2,1)}, u32[]{:S(2)}) copy-start(bf16[2688,16]{0,1:T(8,128)(2,1)} %param.20) | copy-start | bytes 258052
  7.9 7.3 %copy-start.4 = (bf16[2688,16]{0,1:T(8,128)(2,1)S(1)}, bf16[2688,16]{0,1:T(8,128)(2,1)}, u32[]{:S(2)}) copy-start(bf16[2688,16]{0,1:T(8,128)(2,1)} %param.18) | copy-start | bytes 258052
  8.0 7.3 %copy-start.5 = (bf16[2688,16]{0,1:T(8,128)(2,1)S(1)}, bf16[2688,16]{0,1:T(8,128)(2,1)}, u32[]{:S(2)}) copy-start(bf16[2688,16]{0,1:T(8,128)(2,1)} %param.16) | copy-start | bytes 258052
  8.1 19.2 %collective-permute-start.2 = (bf16[1024,512]{1,0:T(8,128)(2,1)S(1)}, bf16[1024,512]{1,0:T(8,128)(2,1)S(1)}, u32[]{:S(2)}, u32[]{:S(2)}) collective-permute-start(bf16[1024,512]{1,0:T(8,128)(2,1)S(1)} %pad_maximum_fusion.1), channel_id=1, source_target_pairs={{0,2},{2,4},{4,6},{6,8},{8,10},{10,12},{12,14},{14,16},{16,18},{18... | collective-permute-start | bytes 3145736 | tf_op jit(solution)/shard_map/ppermute | solution.py:358
  12.4 41.1 %collective-permute-start.3 = (bf16[1024,512]{1,0:T(8,128)(2,1)}, bf16[1024,512]{1,0:T(8,128)(2,1)}, u32[]{:S(2)}, u32[]{:S(2)}) collective-permute-start(bf16[1024,512]{1,0:T(8,128)(2,1)} %pad_maximum_fusion.2), channel_id=1, source_target_pairs={{0,2},{2,4},{4,6},{6,8},{8,10},{10,12},{12,14},{14,16},{16,18},{18... | collective-permute-start | bytes 3145736 | tf_op jit(solution)/shard_map/ppermute | solution.py:358
  16.4 7.5 %collective-permute-start = (f32[48,1024]{1,0:T(8,128)S(1)}, f32[48,1024]{1,0:T(8,128)S(1)}, u32[]{:S(2)}, u32[]{:S(2)}) collective-permute-start(f32[48,1024]{1,0:T(8,128)S(1)} %fusion), channel_id=1, source_target_pairs={{0,1},{1,0},{2,3},{3,2},{4,5},{5,4},{6,7},{7,6},{8,9},{9,8},{10,11... | collective-permute-start | bytes 589832 | tf_op jit(solution)/shard_map/ppermute | solution.py:363
  24.6 2.7 %collective-permute-start.1 = (f32[32,1024]{1,0:T(8,128)S(1)}, f32[32,1024]{1,0:T(8,128)S(1)}, u32[]{:S(2)}, u32[]{:S(2)}) collective-permute-start(f32[32,1024]{1,0:T(8,128)S(1)} %slice.81), channel_id=1, source_target_pairs={{0,2},{2,4},{4,6},{6,8},{8,10},{10,12},{12,14},{14,16},{16,18},{18... | collective-permute-start | bytes 393224 | tf_op jit(solution)/shard_map/ppermute | solution.py:358
  27.9 1.0 copy-start.15
  123.4 31.7 %collective-permute-start.5 = (bf16[32,1024]{1,0:T(8,128)(2,1)}, bf16[32,1024]{1,0:T(8,128)(2,1)S(1)}, u32[]{:S(2)}, u32[]{:S(2)}) collective-permute-start(bf16[32,1024]{1,0:T(8,128)(2,1)} %get-tuple-element.26), channel_id=1, source_target_pairs={{2,0},{4,2},{6,4},{8,6},{10,8},{12,10},{14,12},{16,14},{18,16},{20... | collective-permute-start | bytes 196616 | tf_op jit(solution)/shard_map/ppermute | solution.py:358
  156.0 4.7 %collective-permute-start.6 = (bf16[48,1024]{1,0:T(8,128)(2,1)S(1)}, bf16[48,1024]{1,0:T(8,128)(2,1)S(1)}, u32[]{:S(2)}, u32[]{:S(2)}) collective-permute-start(bf16[48,1024]{1,0:T(8,128)(2,1)S(1)} %fusion.6), channel_id=1, source_target_pairs={{0,1},{1,0},{2,3},{3,2},{4,5},{5,4},{6,7},{7,6},{8,9},{9,8},{10,11... | collective-permute-start | bytes 294920 | tf_op jit(solution)/shard_map/ppermute | solution.py:363
  157.6 7.6 %copy-start.7 = (f32[16,512]{1,0:T(8,128)S(1)}, f32[16,512]{1,0:T(8,128)}, u32[]{:S(2)}) copy-start(f32[16,512]{1,0:T(8,128)} %get-tuple-element.27) | copy-start | bytes 98308
  157.6 7.6 %copy-start.9 = (f32[16,512]{1,0:T(8,128)S(1)}, f32[16,512]{1,0:T(8,128)}, u32[]{:S(2)}) copy-start(f32[16,512]{1,0:T(8,128)} %get-tuple-element.28) | copy-start | bytes 98308
  157.6 7.7 %copy-start.6 = (f32[16,1024]{1,0:T(8,128)S(1)}, f32[16,1024]{1,0:T(8,128)}, u32[]{:S(2)}) copy-start(f32[16,1024]{1,0:T(8,128)} %get-tuple-element.29) | copy-start | bytes 196612
  157.6 7.7 %copy-start.12 = (f32[16,256]{1,0:T(8,128)S(1)}, f32[16,256]{1,0:T(8,128)}, u32[]{:S(2)}) copy-start(f32[16,256]{1,0:T(8,128)} %get-tuple-element.30) | copy-start | bytes 49156
  157.6 7.7 %copy-start.14 = (f32[16,256]{1,0:T(8,128)S(1)}, f32[16,256]{1,0:T(8,128)}, u32[]{:S(2)}) copy-start(f32[16,256]{1,0:T(8,128)} %get-tuple-element.31) | copy-start | bytes 49156
  157.6 7.7 %copy-start.10 = (f32[16,512]{1,0:T(8,128)S(1)}, f32[16,512]{1,0:T(8,128)}, u32[]{:S(2)}) copy-start(f32[16,512]{1,0:T(8,128)} %get-tuple-element.32) | copy-start | bytes 98308
  157.6 7.7 %copy-start.11 = (f32[16,256]{1,0:T(8,128)S(1)}, f32[16,256]{1,0:T(8,128)}, u32[]{:S(2)}) copy-start(f32[16,256]{1,0:T(8,128)} %get-tuple-element.33) | copy-start | bytes 49156
  157.6 7.7 %copy-start.13 = (f32[16,256]{1,0:T(8,128)S(1)}, f32[16,256]{1,0:T(8,128)}, u32[]{:S(2)}) copy-start(f32[16,256]{1,0:T(8,128)} %get-tuple-element.34) | copy-start | bytes 49156
  157.6 7.7 %copy-start.8 = (f32[16,512]{1,0:T(8,128)S(1)}, f32[16,512]{1,0:T(8,128)}, u32[]{:S(2)}) copy-start(f32[16,512]{1,0:T(8,128)} %get-tuple-element.35) | copy-start | bytes 98308
  165.5 3.7 %collective-permute-start.7 = (bf16[16,6144]{1,0:T(8,128)(2,1)S(1)}, bf16[16,6144]{1,0:T(8,128)(2,1)S(1)}, u32[]{:S(2)}, u32[]{:S(2)}) collective-permute-start(bf16[16,6144]{1,0:T(8,128)(2,1)S(1)} %select_convert_fusion), channel_id=1, source_target_pairs={{0,2},{2,0},{4,6},{6,4},{8,10},{10,8},{12,14},{14,12},{16,18},{18,... | collective-permute-start | bytes 589832 | tf_op jit(solution)/shard_map/ppermute | solution.py:363
  169.3 5.8 %collective-permute-start.8 = (bf16[16,3072]{1,0:T(8,128)(2,1)S(1)}, bf16[16,3072]{1,0:T(8,128)(2,1)S(1)}, u32[]{:S(2)}, u32[]{:S(2)}) collective-permute-start(bf16[16,3072]{1,0:T(8,128)(2,1)S(1)} %select_convert_fusion.1), channel_id=1, source_target_pairs={{0,4},{2,6},{4,0},{6,2},{8,12},{10,14},{12,8},{14,10},{16,20},{18,... | collective-permute-start | bytes 294920 | tf_op jit(solution)/shard_map/ppermute | solution.py:363
  175.1 4.9 %collective-permute-start.9 = (bf16[16,3072]{1,0:T(8,128)(2,1)S(1)}, bf16[16,3072]{1,0:T(8,128)(2,1)S(1)}, u32[]{:S(2)}, u32[]{:S(2)}) collective-permute-start(bf16[16,3072]{1,0:T(8,128)(2,1)S(1)} %add_convert_fusion.2), channel_id=1, source_target_pairs={{0,8},{2,10},{4,12},{6,14},{8,0},{10,2},{12,4},{14,6},{16,24},{18,... | collective-permute-start | bytes 294920 | tf_op jit(solution)/shard_map/ppermute | solution.py:363
  180.1 5.7 %collective-permute-start.10 = (bf16[16,3072]{1,0:T(8,128)(2,1)S(1)}, bf16[16,3072]{1,0:T(8,128)(2,1)S(1)}, u32[]{:S(2)}, u32[]{:S(2)}) collective-permute-start(bf16[16,3072]{1,0:T(8,128)(2,1)S(1)} %add_convert_fusion.1), channel_id=1, source_target_pairs={{0,16},{2,18},{4,20},{6,22},{8,24},{10,26},{12,28},{14,30},{16,0},... | collective-permute-start | bytes 294920 | tf_op jit(solution)/shard_map/ppermute | solution.py:363
  185.8 4.7 %collective-permute-start.11 = (bf16[16,3072]{1,0:T(8,128)(2,1)S(1)}, bf16[16,3072]{1,0:T(8,128)(2,1)S(1)}, u32[]{:S(2)}, u32[]{:S(2)}) collective-permute-start(bf16[16,3072]{1,0:T(8,128)(2,1)S(1)} %add_convert_fusion), channel_id=1, source_target_pairs={{0,4},{2,6},{4,0},{6,2},{8,12},{10,14},{12,8},{14,10},{16,20},{18,... | collective-permute-start | bytes 294920 | tf_op jit(solution)/shard_map/ppermute | solution.py:363
  190.5 1.5 collective-permute-start.12
  (2 other events, 1.3 us)
